TPU v7x, 512 devices: a whole 4x8x8 slice. The times are simulated.
512 devices in a mesh: row: 32 (over x, z), col: 16 (over y, core).
Axes of the slice: x: 4, y: 8, z: 8, core: 2. Of those that a mesh axis runs over, the one named last changes fastest.
Arguments:
- c_matrix: float32 [12288, 12288], P('row', 'col'), may hold values from -6 to 6
- a_upper: bfloat16 [12288, 12288], P('row', 'col'), may hold values from -0.3125 to 0.3125
- b_upper: bfloat16 [12288, 12288], P('row', 'col'), may hold values from -0.3125 to 0.3125
- a_vectors: bfloat16 [12288, 384], P('row'), may hold values from -1 to 2, as said below
- a_inverse: bfloat16 [12288, 384], P('row'), may hold values from -1 to 2, as said below
- b_vectors: bfloat16 [12288, 384], P('row'), may hold values from -1 to 2, as said below
- b_inverse: bfloat16 [12288, 384], P('row'), may hold values from -1 to 2, as said below
- a_values: bfloat16 [12288], P('row'), may hold values from 0.5 to 4
- b_values: bfloat16 [12288], P('row'), may hold values from 0.5 to 4
Outputs:
- overwritten: float32 [12288, 12288], P('row', 'col')
Inputs may be any that keep to these rules, and one draw needn't show every extreme that they name: `a_vectors`: each 384 x 384 tile is an identity matrix plus independent entries of deviation about 0.5 / sqrt(384). `a_inverse`: each 384 x 384 tile is an identity matrix plus independent entries of deviation about 0.5 / sqrt(384). `b_vectors`: each 384 x 384 tile is an identity matrix plus independent entries of deviation about 0.5 / sqrt(384). `b_inverse`: each 384 x 384 tile is an identity matrix plus independent entries of deviation about 0.5 / sqrt(384).
All inputs are finite; a program needn't handle non-finite values.
Results may differ from a plain program's by a relative error of at most 0.012.
Values may be sent and summed in bfloat16 or wider, within the bound.
No kernel may reach another device: no remote copies, remote signals or barrier semaphores. Data moves between devices by JAX's collectives and lax.ppermute only.
A program may use at most 64 MiB of HBM per device.

v0:
```python
import jax
import jax.numpy as jnp
from jax import lax
from jax.experimental import pallas as pl
from jax.experimental.pallas import tpu as pltpu
from jax.sharding import PartitionSpec as P

ROWS, COLS = 32, 16


def send(x, pairs):
    flat = [(a * COLS + b, c * COLS + d) for (a, b), (c, d) in pairs]
    return lax.ppermute(x, ("row", "col"), flat)


def band(offsets, rows, cols):
    pairs = []
    for c in range(COLS):
        for d in offsets:
            r = 2 * c + d
            if 0 <= r < ROWS and 0 <= r + rows < ROWS and 0 <= c + cols < COLS:
                pairs.append(((r, c), (r + rows, c + cols)))
    return pairs


def dot(a, b):
    return jnp.dot(a, b, preferred_element_type=jnp.float32)


def solve(residue, left, right):
    left_vectors, left_inverse, left_values = left
    right_packed, right_inverse = right
    tile = residue.shape[0]
    first = dot(left_inverse[...], residue.astype(jnp.bfloat16)).astype(jnp.bfloat16)
    second = dot(first, right_packed[:tile, :])
    right_values = right_packed[tile:, :].astype(jnp.float32)[:1]
    third = (second / (left_values[...] + right_values)).astype(jnp.bfloat16)
    fourth = dot(left_vectors[...], third).astype(jnp.bfloat16)
    return dot(fourth, right_inverse[...])


def tile_of(ref, slot):
    tile = ref.shape[0]
    return ref[:, pl.ds(pl.multiple_of(slot * tile, tile), tile)]


def either(condition, first, second):
    chosen = jnp.where(condition, first.astype(jnp.float32), second.astype(jnp.float32))
    return chosen.astype(jnp.bfloat16)


def first_wave(info, c, u, p, lam, vm, q, x, xb):
    value = solve(tile_of(c, info[0]), (u, p, lam), (vm, q))
    x[...] = value
    xb[...] = value.astype(jnp.bfloat16)


def second_wave(info, c, n, below, across, own, b_band, u, p, lam, vm, q, x, xb):
    slot = info[1]
    left = either(slot == 0, across[...], own[...])
    residue = tile_of(c, slot) - dot(tile_of(n, slot), below[...]) - dot(left, tile_of(b_band, slot))
    value = solve(residue, (u, p, lam), (vm, q))
    x[...] = value
    xb[...] = value.astype(jnp.bfloat16)


def third_wave(
    info, c, a, n, col_two, row_two, col_one, row_one, own, b_band, b_above, u, p, lam, vm, q,
    x, down, across,
):
    slot = info[2]
    tile = x.shape[0]
    left = either(slot == 0, row_one[...], own[...])
    a_tile = either(slot == 0, a[:, tile:], n[:, :tile])
    residue = (
        tile_of(c, slot)
        - dot(tile_of(n, slot), col_two[...])
        - dot(row_two[...], tile_of(b_band, slot))
        - dot(a_tile, col_one[...])
        - dot(left, tile_of(b_above, slot))
    )
    value = solve(residue, (u, p, lam), (vm, q))
    x[...] = value
    packed = value.astype(jnp.bfloat16)
    down[0] = col_one[...]
    down[1] = packed
    across[0] = left
    across[1] = packed


def last_update(
    info, c, a, n, b, b_above, b_above_two, down_two, down, row_two, across, x_two, x_one, x_zero, out
):
    tile = c.shape[0]
    a_tiles = (a.at[:, :tile], a.at[:, tile:], n.at[:, :tile], n.at[:, tile:])
    for member in range(2):
        where = info[3] - member
        span = slice(member * tile, (member + 1) * tile)

        @pl.when(where < 0)
        def _():
            change = dot(a_tiles[member][...], down[member, 1])
            change += dot(a_tiles[member + 1][...], down[member, 0])
            change += dot(a_tiles[member + 2][...], down_two[member, 0])
            change += dot(across[1], b[:, span])
            change += dot(across[0], b_above[:, span])
            change += dot(row_two[0], b_above_two[:, span])
            out[:, span] = c[:, span] - change

        for wave, solved in enumerate((x_zero, x_one, x_two)):

            @pl.when(where == wave)
            def _():
                out[:, span] = solved[...]

        @pl.when(where > 2)
        def _():
            out[:, span] = c[:, span]


def run(kernel, outs, dots, info, *operands):
    tile = operands[0].shape[0]
    moved = sum(v.size * v.dtype.itemsize for v in (*operands, *outs))
    whole = pl.BlockSpec(memory_space=pltpu.VMEM)
    return pl.pallas_call(
        kernel,
        out_shape=outs,
        in_specs=[pl.BlockSpec(memory_space=pltpu.SMEM)] + [whole] * len(operands),
        out_specs=[whole] * len(outs),
        cost_estimate=pl.CostEstimate(
            flops=2 * dots * tile**3, bytes_accessed=moved, transcendentals=0
        ),
    )(info, *operands)


def row_tree(x, offset):
    chips = offset // 2
    for step in (4, 2, 1):
        pairs = []
        for k in range(ROWS):
            for away in range(0, 8, 2 * step):
                c = k // 2 + 2 * away
                if c + 2 * step < COLS:
                    pairs.append(((k, c), (k, c + 2 * step)))
        got = send(x, pairs)
        takes = (offset % 2 == 0) & (chips % (2 * step) == step)
        x = jnp.where(takes, got, x)
    pairs = []
    for k in range(ROWS):
        for c in range(k // 2, COLS, 2):
            if (c ^ 1) > k // 2:
                pairs.append(((k, c), (k, c ^ 1)))
    got = send(x, pairs)
    return jnp.where(offset % 2 == 0, x, got)


def col_spread(x, row, col):
    tile = x.shape[1]
    plane, z = row // 8, row % 8
    relative = plane ^ (col // 4)
    half, quarter = tile // 2, tile // 4
    diagonal = [(k // 8, k % 8, k // 2) for k in range(ROWS)]
    got = send(x[:, half:], [((p * 8 + s, c), ((3 - p) * 8 + s, c)) for p, s, c in diagonal])
    part = jnp.where(relative == 0, x[:, :half], got)
    pairs = []
    for p, s, c in diagonal:
        pairs.append(((p * 8 + s, c), ((p ^ 1) * 8 + s, c)))
        pairs.append((((3 - p) * 8 + s, c), (((3 - p) ^ 1) * 8 + s, c)))
    got = send(part[:, quarter:], pairs)
    first = (relative == 0) | (relative == 3)
    part = jnp.where(first, part[:, :quarter], got)
    source = (col % 4) // 2
    base = 2 * (col % 4)
    pairs = [((q * 8 + s, c), (q * 8 + 7 - s, c)) for _, s, c in diagonal for q in range(4)]
    got = send(part, pairs)
    part = jnp.where((z // 2) * 2 == base, part, got)
    pairs = []
    for _, s, c in diagonal:
        for q in range(4):
            for t in (s, 7 - s):
                pairs.append(((q * 8 + t, c), (q * 8 + (t ^ 2), c)))
    got = send(part, pairs)
    holds = ((z // 2) * 2 == base) | (((7 - z) // 2) * 2 == base)
    part = jnp.where(holds, part, got)
    every = [(r, c) for r in range(ROWS) for c in range(COLS)]
    got = send(part, [((r, c), (r ^ 1, c)) for r, c in every])
    is_second = (z % 2) ^ ((z // 4) != source).astype(jnp.int32)
    both = jnp.stack([jnp.where(is_second == 0, part, got), jnp.where(is_second == 0, got, part)])
    got = send(both, [((r, c), (r ^ 8, c)) for r, c in every])
    both = jnp.concatenate([jnp.where(first, both, got), jnp.where(first, got, both)], axis=2)
    got = send(both, [((r, c), (r ^ 24, c)) for r, c in every])
    upper = relative <= 1
    return jnp.concatenate([jnp.where(upper, both, got), jnp.where(upper, got, both)], axis=2)


def shards(
    c_matrix, a_upper, b_upper, a_vectors, a_inverse, b_vectors, b_inverse, a_values, b_values
):
    tile = a_vectors.shape[1]
    row = lax.axis_index("row")
    col = lax.axis_index("col")
    d = row - 2 * col
    info = jnp.stack([jnp.clip(d - 2, 0, 1), jnp.clip(d - 1, 0, 1), jnp.clip(d, 0, 1), d])
    left = (a_vectors, a_inverse, a_values.astype(jnp.float32)[:, None])
    square = jax.ShapeDtypeStruct((tile, tile), jnp.bfloat16)
    exact = jax.ShapeDtypeStruct((tile, tile), jnp.float32)
    pair = jax.ShapeDtypeStruct((2, tile, tile), jnp.bfloat16)

    packed = jnp.concatenate([b_vectors, jnp.broadcast_to(b_values[None], (16, tile))])
    packed_one = send(packed, band((0, 1), 1, 0))
    inverse_one = send(b_inverse, band((0, 1), 1, 0))
    packed_two = send(packed_one, band((1, 2), 1, 0))
    inverse_two = send(inverse_one, band((1, 2), 1, 0))
    b_band = send(b_upper, band((-2, -1, 0), 2, 0))
    a_next = send(a_upper, [((r, c), (r, c - 1)) for r in range(ROWS) for c in range(1, COLS)])

    def rows_down(last):
        rows = range(ROWS - 1)
        return [((r, c), (r + 1, c)) for r in rows for c in range(COLS) if r + 1 <= 2 * c + last]

    b_above = send(b_upper, rows_down(1))
    b_above_two = send(b_above, rows_down(0))

    x_two, solved_two = run(first_wave, (exact, square), 4, info, c_matrix, *left, packed_two, inverse_two)
    below = send(solved_two, band((2, 3), -1, 0))
    row_two = send(solved_two, band((2, 3), 0, 1))
    col_two = send(solved_two, band((2, 3), -2, 0))
    x_one, solved_one = run(
        second_wave, (exact, square), 6, info,
        c_matrix, a_next, below, row_two, solved_two, b_band, *left, packed_one, inverse_one,
    )
    col_one = send(solved_one, band((1, 2), -1, 0))
    row_one = send(solved_one, band((2,), 0, 1))
    x_zero, down, across = run(
        third_wave, (exact, pair, pair), 8, info,
        c_matrix, a_upper, a_next, col_two, row_two, col_one, row_one, solved_one,
        b_band, b_above, *left, packed, b_inverse,
    )
    offset = col - row // 2
    down_two = col_spread(col_two[None], row, col)
    across_two = row_tree(row_two[None], offset)
    down = col_spread(down, row, col)
    across = row_tree(across, offset)
    return run(
        last_update, (jax.ShapeDtypeStruct(c_matrix.shape, jnp.float32),), 12, info,
        c_matrix, a_upper, a_next, b_upper, b_above, b_above_two,
        down_two, down, across_two, across, x_two, x_one, x_zero,
    )[0]


def solution(mesh):
    placed = (
        P("row", "col"),
        P("row", "col"),
        P("row", "col"),
        P("row", None),
        P("row", None),
        P("row", None),
        P("row", None),
        P("row"),
        P("row"),
    )

    return jax.shard_map(shards, mesh=mesh, in_specs=placed, out_specs=P("row", "col"), check_vma=False)
```

profile of v0, /device:TPU:152, one launch (start us, length us, event | category | flops | bytes accessed | tf_op | source)
XLA Modules:
  0.0 168.4 jit_solution(14053568303554844721)
XLA Ops:
  4.5 1.5 reshape.2.lam
  8.1 3.8 %shard_map.91 = (f32[384,384]{1,0:T(8,128)}, bf16[384,384]{1,0:T(8,128)(2,1)}) custom-call(s32[4]{0:T(128)} %pad_add_fusion.info, f32[384,768]{1,0:T(8,128)} %c.7, bf16[384,384]{1,0:T(8,128)(2,1)} %u.5, bf16[384,384]{1,0:T(8,128)(2,1)} %p.5, f32[384,1]{1,0:T(8,128)} %reshape.2.lam, bf16[400,384]{1,0:T(8,128)(2,1)} %copy-done.14, bf16[384,384]{1,0:T(8,128)(2,1)} %copy-done.18), custom_call_target="tpu_custom_call" | custom-call | flops 452984832 | bytes 3257856 | tf_op jit(solution)/shard_map/pallas_call | solution.py:125
  14.0 4.3 %collective-permute-start.1 = (bf16[384,768]{1,0:T(8,128)(2,1)S(1)}, bf16[384,768]{1,0:T(8,128)(2,1)S(1)}, u32[]{:S(2)}, u32[]{:S(2)}) collective-permute-start(bf16[384,768]{1,0:T(8,128)(2,1)S(1)} %copy-done.8), channel_id=1, source_target_pairs={{0,16},{1,17},{2,18},{3,19},{4,20},{5,21},{6,22},{7,23},{8,24},{9,... | collective-permute-start | bytes 1769480 | tf_op jit(solution)/shard_map/ppermute | solution.py:13
  18.3 1.9 %collective-permute-start = (bf16[384,768]{1,0:T(8,128)(2,1)S(1)}, bf16[384,768]{1,0:T(8,128)(2,1)S(1)}, u32[]{:S(2)}, u32[]{:S(2)}) collective-permute-start(bf16[384,768]{1,0:T(8,128)(2,1)S(1)} %copy-done.3), channel_id=1, source_target_pairs={{1,0},{2,1},{3,2},{4,3},{5,4},{6,5},{7,6},{8,7},{9,8},{10,9},{11,1... | collective-permute-start | bytes 1769480 | tf_op jit(solution)/shard_map/ppermute | solution.py:13
  22.9 1.4 collective-permute-start.16
  24.3 1.6 slice_select_fusion.3
  25.9 1.7 %collective-permute-done.n = bf16[384,768]{1,0:T(8,128)(2,1)S(1)} collective-permute-done((bf16[384,768]{1,0:T(8,128)(2,1)S(1)}, bf16[384,768]{1,0:T(8,128)(2,1)S(1)}, u32[]{:S(2)}, u32[]{:S(2)}) %collective-permute-start) | collective-permute-done | bytes 589856 | tf_op jit(solution)/shard_map/ppermute | solution.py:13
  29.8 4.8 %shard_map.92 = (f32[384,384]{1,0:T(8,128)}, bf16[384,384]{1,0:T(8,128)(2,1)}) custom-call(s32[4]{0:T(128)} %pad_add_fusion.info, f32[384,768]{1,0:T(8,128)} %c.7, bf16[384,768]{1,0:T(8,128)(2,1)} %copy-done, bf16[384,384]{1,0:T(8,128)(2,1)} %collective-permute-done.16.below, bf16[384,384]{1,0:T(8,128)(2,1)} %copy-done.1, ...), custom_call_target="tpu_custom_call" | custom-call | flops 679477248 | bytes 5322240 | tf_op jit(solution)/shard_map/pallas_call | solution.py:125
  36.3 5.5 %collective-permute-start.2 = (bf16[384,768]{1,0:T(8,128)(2,1)S(1)}, bf16[384,768]{1,0:T(8,128)(2,1)S(1)}, u32[]{:S(2)}, u32[]{:S(2)}) collective-permute-start(bf16[384,768]{1,0:T(8,128)(2,1)S(1)} %collective-permute-done.1.b_above), channel_id=1, source_target_pairs={{1,17},{2,18},{3,19},{4,20},{5,21},{6,22},{7,23},{8,24},{9,25},{10... | collective-permute-start | bytes 1769480 | tf_op jit(solution)/shard_map/ppermute | solution.py:13
  42.4 18.8 %collective-permute-done.10 = bf16[1,96,384]{2,1,0:T(8,128)(2,1)S(1)} collective-permute-done((bf16[1,96,384]{2,1,0:T(8,128)(2,1)}, bf16[1,96,384]{2,1,0:T(8,128)(2,1)S(1)}, u32[]{:S(2)}, u32[]{:S(2)}) %collective-permute-start.10) | collective-permute-done | bytes 73760 | tf_op jit(solution)/shard_map/ppermute | solution.py:13
  61.3 1.4 collective-permute-start.11
  64.2 6.1 %shard_map.93 = (f32[384,384]{1,0:T(8,128)}, bf16[2,384,384]{2,1,0:T(8,128)(2,1)}, bf16[2,384,384]{2,1,0:T(8,128)(2,1)}) custom-call(s32[4]{0:T(128)} %pad_add_fusion.info, f32[384,768]{1,0:T(8,128)} %c.7, bf16[384,768]{1,0:T(8,128)(2,1)} %a.3, bf16[384,768]{1,0:T(8,128)(2,1)} %copy-done, bf16[384,384]{1,0:T(8,128)(2,1)} %copy-done.7, ...), custom_call_target="tpu_custom_call" | custom-call | flops 905969664 | bytes 7976448 | tf_op jit(solution)/shard_map/pallas_call | solution.py:125
  71.2 13.2 %collective-permute-start.12 = (bf16[1,96,384]{2,1,0:T(8,128)(2,1)S(1)}, bf16[1,96,384]{2,1,0:T(8,128)(2,1)S(1)}, u32[]{:S(2)}, u32[]{:S(2)}) collective-permute-start(bf16[1,96,384]{2,1,0:T(8,128)(2,1)S(1)} %broadcast_select_fusion.19), channel_id=1, source_target_pairs={{0,16},{1,17},{2,18},{3,19},{4,20},{5,21},{6,22},{7,23},{8,24},{9,... | collective-permute-start | bytes 221192 | tf_op jit(solution)/shard_map/ppermute | solution.py:13
  86.7 14.7 %collective-permute-start.13 = (bf16[2,1,96,384]{3,2,1,0:T(8,128)(2,1)S(1)}, bf16[2,1,96,384]{3,2,1,0:T(8,128)(2,1)S(1)}, u32[]{:S(2)}, u32[]{:S(2)}) collective-permute-start(bf16[2,1,96,384]{3,2,1,0:T(8,128)(2,1)S(1)} %pad_maximum_fusion.6), channel_id=1, source_target_pairs={{0,128},{1,129},{2,130},{3,131},{4,132},{5,133},{6,134},{7,135},{8... | collective-permute-start | bytes 442376 | tf_op jit(solution)/shard_map/ppermute | solution.py:13
  105.5 1.9 %collective-permute-start.14 = (bf16[2,1,192,384]{3,2,1,0:T(8,128)(2,1)S(1)}, bf16[2,1,192,384]{3,2,1,0:T(8,128)(2,1)S(1)}, u32[]{:S(2)}, u32[]{:S(2)}) collective-permute-start(bf16[2,1,192,384]{3,2,1,0:T(8,128)(2,1)S(1)} %pad_maximum_fusion.4), channel_id=1, source_target_pairs={{0,384},{1,385},{2,386},{3,387},{4,388},{5,389},{6,390},{7,391},{8... | collective-permute-start | bytes 884744 | tf_op jit(solution)/shard_map/ppermute | solution.py:13
  107.4 9.2 %collective-permute-done.22 = bf16[2,96,384]{2,1,0:T(8,128)(2,1)S(1)} collective-permute-done((bf16[2,96,384]{2,1,0:T(8,128)(2,1)S(1)}, bf16[2,96,384]{2,1,0:T(8,128)(2,1)S(1)}, u32[]{:S(2)}, u32[]{:S(2)}) %collective-permute-start.22) | collective-permute-done | bytes 147488 | tf_op jit(solution)/shard_map/ppermute | solution.py:13
  118.8 3.4 %collective-permute-done.23 = bf16[2,96,384]{2,1,0:T(8,128)(2,1)S(1)} collective-permute-done((bf16[2,96,384]{2,1,0:T(8,128)(2,1)S(1)}, bf16[2,96,384]{2,1,0:T(8,128)(2,1)S(1)}, u32[]{:S(2)}, u32[]{:S(2)}) %collective-permute-start.23) | collective-permute-done | bytes 147488 | tf_op jit(solution)/shard_map/ppermute | solution.py:13
  122.2 1.9 %collective-permute-start.24 = (bf16[2,96,384]{2,1,0:T(8,128)(2,1)S(1)}, bf16[2,96,384]{2,1,0:T(8,128)(2,1)S(1)}, u32[]{:S(2)}, u32[]{:S(2)}) collective-permute-start(bf16[2,96,384]{2,1,0:T(8,128)(2,1)S(1)} %broadcast_select_fusion.15), channel_id=1, source_target_pairs={{0,16},{1,17},{2,18},{3,19},{4,20},{5,21},{6,22},{7,23},{8,24},{9,... | collective-permute-start | bytes 442376 | tf_op jit(solution)/shard_map/ppermute | solution.py:13
  125.5 4.9 %collective-permute-done.24 = bf16[2,96,384]{2,1,0:T(8,128)(2,1)S(1)} collective-permute-done((bf16[2,96,384]{2,1,0:T(8,128)(2,1)S(1)}, bf16[2,96,384]{2,1,0:T(8,128)(2,1)S(1)}, u32[]{:S(2)}, u32[]{:S(2)}) %collective-permute-start.24) | collective-permute-done | bytes 147488 | tf_op jit(solution)/shard_map/ppermute | solution.py:13
  130.5 1.9 %collective-permute-start.25 = (bf16[2,2,96,384]{3,2,1,0:T(8,128)(2,1)S(1)}, bf16[2,2,96,384]{3,2,1,0:T(8,128)(2,1)S(1)}, u32[]{:S(2)}, u32[]{:S(2)}) collective-permute-start(bf16[2,2,96,384]{3,2,1,0:T(8,128)(2,1)S(1)} %pad_maximum_fusion.5), channel_id=1, source_target_pairs={{0,128},{1,129},{2,130},{3,131},{4,132},{5,133},{6,134},{7,135},{8... | collective-permute-start | bytes 884744 | tf_op jit(solution)/shard_map/ppermute | solution.py:13
  133.3 7.6 %collective-permute-done.25 = bf16[2,2,96,384]{3,2,1,0:T(8,128)(2,1)S(1)} collective-permute-done((bf16[2,2,96,384]{3,2,1,0:T(8,128)(2,1)S(1)}, bf16[2,2,96,384]{3,2,1,0:T(8,128)(2,1)S(1)}, u32[]{:S(2)}, u32[]{:S(2)}) %collective-permute-start.25) | collective-permute-done | bytes 294944 | tf_op jit(solution)/shard_map/ppermute | solution.py:13
  141.1 2.2 %collective-permute-start.26 = (bf16[2,2,192,384]{3,2,1,0:T(8,128)(2,1)S(1)}, bf16[2,2,192,384]{3,2,1,0:T(8,128)(2,1)S(1)}, u32[]{:S(2)}, u32[]{:S(2)}) collective-permute-start(bf16[2,2,192,384]{3,2,1,0:T(8,128)(2,1)S(1)} %pad_maximum_fusion.2), channel_id=1, source_target_pairs={{0,384},{1,385},{2,386},{3,387},{4,388},{5,389},{6,390},{7,391},{8... | collective-permute-start | bytes 1769480 | tf_op jit(solution)/shard_map/ppermute | solution.py:13
  146.3 11.9 %collective-permute-done.26 = bf16[2,2,192,384]{3,2,1,0:T(8,128)(2,1)S(1)} collective-permute-done((bf16[2,2,192,384]{3,2,1,0:T(8,128)(2,1)S(1)}, bf16[2,2,192,384]{3,2,1,0:T(8,128)(2,1)S(1)}, u32[]{:S(2)}, u32[]{:S(2)}) %collective-permute-start.26) | collective-permute-done | bytes 589856 | tf_op jit(solution)/shard_map/ppermute | solution.py:13
  161.4 6.9 %shard_map.94 = f32[384,768]{1,0:T(8,128)} custom-call(s32[4]{0:T(128)} %pad_add_fusion.info, f32[384,768]{1,0:T(8,128)} %c.7, bf16[384,768]{1,0:T(8,128)(2,1)} %a.3, bf16[384,768]{1,0:T(8,128)(2,1)} %copy-done, bf16[384,768]{1,0:T(8,128)(2,1)} %b.1, bf16[384,768]{1,0:T(8,128)(2,1)} %copy-done.4, bf16[384,768]{1,0:T(8,128)(2,1)} %copy-done.9, ...), custom_call_target="tpu_custom_call" | custom-call | flops 1358954496 | bytes 9732096 | tf_op jit(solution)/shard_map/pallas_call | solution.py:125
  (124 shorter events, 34.8 us)
Async XLA Ops:
  13.3 15.6 %collective-permute-start.17 = (bf16[384,768]{1,0:T(8,128)(2,1)S(1)}, bf16[384,768]{1,0:T(8,128)(2,1)S(1)}, u32[]{:S(2)}, u32[]{:S(2)}) collective-permute-start(bf16[384,768]{1,0:T(8,128)(2,1)S(1)} %copy-done.8), channel_id=1, source_target_pairs={{0,32},{1,33},{17,49},{33,65},{34,66},{50,82},{66,98},{67,99},{83,... | collective-permute-start | bytes 1769480 | tf_op jit(solution)/shard_map/ppermute | solution.py:13
  14.0 22.2 %collective-permute-start.1 = (bf16[384,768]{1,0:T(8,128)(2,1)S(1)}, bf16[384,768]{1,0:T(8,128)(2,1)S(1)}, u32[]{:S(2)}, u32[]{:S(2)}) collective-permute-start(bf16[384,768]{1,0:T(8,128)(2,1)S(1)} %copy-done.8), channel_id=1, source_target_pairs={{0,16},{1,17},{2,18},{3,19},{4,20},{5,21},{6,22},{7,23},{8,24},{9,... | collective-permute-start | bytes 1769480 | tf_op jit(solution)/shard_map/ppermute | solution.py:13
  18.3 9.3 %collective-permute-start = (bf16[384,768]{1,0:T(8,128)(2,1)S(1)}, bf16[384,768]{1,0:T(8,128)(2,1)S(1)}, u32[]{:S(2)}, u32[]{:S(2)}) collective-permute-start(bf16[384,768]{1,0:T(8,128)(2,1)S(1)} %copy-done.3), channel_id=1, source_target_pairs={{1,0},{2,1},{3,2},{4,3},{5,4},{6,5},{7,6},{8,7},{9,8},{10,9},{11,1... | collective-permute-start | bytes 1769480 | tf_op jit(solution)/shard_map/ppermute | solution.py:13
  27.6 33.6 %collective-permute-start.10 = (bf16[1,96,384]{2,1,0:T(8,128)(2,1)}, bf16[1,96,384]{2,1,0:T(8,128)(2,1)S(1)}, u32[]{:S(2)}, u32[]{:S(2)}) collective-permute-start(bf16[1,96,384]{2,1,0:T(8,128)(2,1)} %slice_select_fusion.3), channel_id=1, source_target_pairs={{0,112},{128,240},{256,368},{384,496},{16,96},{144,224},{272,352},... | collective-permute-start | bytes 221192 | tf_op jit(solution)/shard_map/ppermute | solution.py:13
  34.6 28.1 %collective-permute-start.18 = (bf16[384,384]{1,0:T(8,128)(2,1)}, bf16[384,384]{1,0:T(8,128)(2,1)S(1)}, u32[]{:S(2)}, u32[]{:S(2)}) collective-permute-start(bf16[384,384]{1,0:T(8,128)(2,1)} %get-tuple-element.13.own), channel_id=1, source_target_pairs={{16,0},{32,16},{49,33},{65,49},{82,66},{98,82},{115,99},{131,115},... | collective-permute-start | bytes 884744 | tf_op jit(solution)/shard_map/ppermute | solution.py:13
  35.3 27.4 %collective-permute-start.19 = (bf16[384,384]{1,0:T(8,128)(2,1)}, bf16[384,384]{1,0:T(8,128)(2,1)S(1)}, u32[]{:S(2)}, u32[]{:S(2)}) collective-permute-start(bf16[384,384]{1,0:T(8,128)(2,1)} %get-tuple-element.13.own), channel_id=1, source_target_pairs={{32,33},{65,66},{98,99},{131,132},{164,165},{197,198},{230,231},{2... | collective-permute-start | bytes 884744 | tf_op jit(solution)/shard_map/ppermute | solution.py:13
  36.3 124.3 %collective-permute-start.2 = (bf16[384,768]{1,0:T(8,128)(2,1)S(1)}, bf16[384,768]{1,0:T(8,128)(2,1)S(1)}, u32[]{:S(2)}, u32[]{:S(2)}) collective-permute-start(bf16[384,768]{1,0:T(8,128)(2,1)S(1)} %collective-permute-done.1.b_above), channel_id=1, source_target_pairs={{1,17},{2,18},{3,19},{4,20},{5,21},{6,22},{7,23},{8,24},{9,25},{10... | collective-permute-start | bytes 1769480 | tf_op jit(solution)/shard_map/ppermute | solution.py:13
  41.7 42.6 %collective-permute-start.27 = (bf16[1,384,384]{2,1,0:T(8,128)(2,1)}, bf16[1,384,384]{2,1,0:T(8,128)(2,1)S(1)}, u32[]{:S(2)}, u32[]{:S(2)}) collective-permute-start(bf16[1,384,384]{2,1,0:T(8,128)(2,1)} %bitcast.15), channel_id=1, source_target_pairs={{0,8},{16,24},{33,41},{49,57},{66,74},{82,90},{99,107},{115,123},{... | collective-permute-start | bytes 884744 | tf_op jit(solution)/shard_map/ppermute | solution.py:13
  61.3 9.8 %collective-permute-start.11 = (bf16[1,96,384]{2,1,0:T(8,128)(2,1)S(1)}, bf16[1,96,384]{2,1,0:T(8,128)(2,1)S(1)}, u32[]{:S(2)}, u32[]{:S(2)}) collective-permute-start(bf16[1,96,384]{2,1,0:T(8,128)(2,1)S(1)} %broadcast_select_fusion.18), channel_id=1, source_target_pairs={{0,32},{112,80},{128,160},{240,208},{256,288},{368,336},{384,416},... | collective-permute-start | bytes 221192 | tf_op jit(solution)/shard_map/ppermute | solution.py:13
  70.3 47.7 %collective-permute-start.31 = (bf16[2,384,384]{2,1,0:T(8,128)(2,1)}, bf16[2,384,384]{2,1,0:T(8,128)(2,1)S(1)}, u32[]{:S(2)}, u32[]{:S(2)}) collective-permute-start(bf16[2,384,384]{2,1,0:T(8,128)(2,1)} %get-tuple-element.15), channel_id=1, source_target_pairs={{0,8},{16,24},{33,41},{49,57},{66,74},{82,90},{99,107},{115,123},{... | collective-permute-start | bytes 1769480 | tf_op jit(solution)/shard_map/ppermute | solution.py:13
  71.2 15.5 %collective-permute-start.12 = (bf16[1,96,384]{2,1,0:T(8,128)(2,1)S(1)}, bf16[1,96,384]{2,1,0:T(8,128)(2,1)S(1)}, u32[]{:S(2)}, u32[]{:S(2)}) collective-permute-start(bf16[1,96,384]{2,1,0:T(8,128)(2,1)S(1)} %broadcast_select_fusion.19), channel_id=1, source_target_pairs={{0,16},{1,17},{2,18},{3,19},{4,20},{5,21},{6,22},{7,23},{8,24},{9,... | collective-permute-start | bytes 221192 | tf_op jit(solution)/shard_map/ppermute | solution.py:13
  84.4 17.7 %collective-permute-start.28 = (bf16[1,384,384]{2,1,0:T(8,128)(2,1)S(1)}, bf16[1,384,384]{2,1,0:T(8,128)(2,1)S(1)}, u32[]{:S(2)}, u32[]{:S(2)}) collective-permute-start(bf16[1,384,384]{2,1,0:T(8,128)(2,1)S(1)} %broadcast_select_fusion.6), channel_id=1, source_target_pairs={{0,4},{8,12},{16,20},{24,28},{33,37},{41,45},{49,53},{57,61},{66,7... | collective-permute-start | bytes 884744 | tf_op jit(solution)/shard_map/ppermute | solution.py:13
  85.1 16.2 %collective-permute-start.20 = (bf16[2,192,384]{2,1,0:T(8,128)(2,1)S(1)}, bf16[2,192,384]{2,1,0:T(8,128)(2,1)S(1)}, u32[]{:S(2)}, u32[]{:S(2)}) collective-permute-start(bf16[2,192,384]{2,1,0:T(8,128)(2,1)S(1)} %slice.29), channel_id=1, source_target_pairs={{0,384},{16,400},{33,417},{49,433},{66,450},{82,466},{99,483},{115... | collective-permute-start | bytes 884744 | tf_op jit(solution)/shard_map/ppermute | solution.py:13
  86.7 18.7 %collective-permute-start.13 = (bf16[2,1,96,384]{3,2,1,0:T(8,128)(2,1)S(1)}, bf16[2,1,96,384]{3,2,1,0:T(8,128)(2,1)S(1)}, u32[]{:S(2)}, u32[]{:S(2)}) collective-permute-start(bf16[2,1,96,384]{3,2,1,0:T(8,128)(2,1)S(1)} %pad_maximum_fusion.6), channel_id=1, source_target_pairs={{0,128},{1,129},{2,130},{3,131},{4,132},{5,133},{6,134},{7,135},{8... | collective-permute-start | bytes 442376 | tf_op jit(solution)/shard_map/ppermute | solution.py:13
  102.2 21.9 %collective-permute-start.29 = (bf16[1,384,384]{2,1,0:T(8,128)(2,1)S(1)}, bf16[1,384,384]{2,1,0:T(8,128)(2,1)S(1)}, u32[]{:S(2)}, u32[]{:S(2)}) collective-permute-start(bf16[1,384,384]{2,1,0:T(8,128)(2,1)S(1)} %broadcast_select_fusion.7), channel_id=1, source_target_pairs={{0,2},{4,6},{8,10},{12,14},{16,18},{20,22},{24,26},{28,30},{33,35}... | collective-permute-start | bytes 884744 | tf_op jit(solution)/shard_map/ppermute | solution.py:13
  103.1 13.6 %collective-permute-start.22 = (bf16[2,96,384]{2,1,0:T(8,128)(2,1)S(1)}, bf16[2,96,384]{2,1,0:T(8,128)(2,1)S(1)}, u32[]{:S(2)}, u32[]{:S(2)}) collective-permute-start(bf16[2,96,384]{2,1,0:T(8,128)(2,1)S(1)} %slice_select_fusion.1), channel_id=1, source_target_pairs={{0,112},{128,240},{256,368},{384,496},{16,96},{144,224},{272,352},... | collective-permute-start | bytes 442376 | tf_op jit(solution)/shard_map/ppermute | solution.py:13
  105.5 27.7 %collective-permute-start.14 = (bf16[2,1,192,384]{3,2,1,0:T(8,128)(2,1)S(1)}, bf16[2,1,192,384]{3,2,1,0:T(8,128)(2,1)S(1)}, u32[]{:S(2)}, u32[]{:S(2)}) collective-permute-start(bf16[2,1,192,384]{3,2,1,0:T(8,128)(2,1)S(1)} %pad_maximum_fusion.4), channel_id=1, source_target_pairs={{0,384},{1,385},{2,386},{3,387},{4,388},{5,389},{6,390},{7,391},{8... | collective-permute-start | bytes 884744 | tf_op jit(solution)/shard_map/ppermute | solution.py:13
  118.1 14.3 %collective-permute-start.32 = (bf16[2,384,384]{2,1,0:T(8,128)(2,1)S(1)}, bf16[2,384,384]{2,1,0:T(8,128)(2,1)S(1)}, u32[]{:S(2)}, u32[]{:S(2)}) collective-permute-start(bf16[2,384,384]{2,1,0:T(8,128)(2,1)S(1)} %broadcast_select_fusion), channel_id=1, source_target_pairs={{0,4},{8,12},{16,20},{24,28},{33,37},{41,45},{49,53},{57,61},{66,7... | collective-permute-start | bytes 1769480 | tf_op jit(solution)/shard_map/ppermute | solution.py:13
  122.2 8.2 %collective-permute-start.24 = (bf16[2,96,384]{2,1,0:T(8,128)(2,1)S(1)}, bf16[2,96,384]{2,1,0:T(8,128)(2,1)S(1)}, u32[]{:S(2)}, u32[]{:S(2)}) collective-permute-start(bf16[2,96,384]{2,1,0:T(8,128)(2,1)S(1)} %broadcast_select_fusion.15), channel_id=1, source_target_pairs={{0,16},{1,17},{2,18},{3,19},{4,20},{5,21},{6,22},{7,23},{8,24},{9,... | collective-permute-start | bytes 442376 | tf_op jit(solution)/shard_map/ppermute | solution.py:13
  124.2 21.4 %collective-permute-start.30 = (bf16[1,384,384]{2,1,0:T(8,128)(2,1)S(1)}, bf16[1,384,384]{2,1,0:T(8,128)(2,1)S(1)}, u32[]{:S(2)}, u32[]{:S(2)}) collective-permute-start(bf16[1,384,384]{2,1,0:T(8,128)(2,1)S(1)} %broadcast_select_fusion.8), channel_id=1, source_target_pairs={{0,1},{2,3},{4,5},{6,7},{8,9},{10,11},{12,13},{14,15},{16,17},{18,... | collective-permute-start | bytes 884744 | tf_op jit(solution)/shard_map/ppermute | solution.py:13
  130.5 10.5 %collective-permute-start.25 = (bf16[2,2,96,384]{3,2,1,0:T(8,128)(2,1)S(1)}, bf16[2,2,96,384]{3,2,1,0:T(8,128)(2,1)S(1)}, u32[]{:S(2)}, u32[]{:S(2)}) collective-permute-start(bf16[2,2,96,384]{3,2,1,0:T(8,128)(2,1)S(1)} %pad_maximum_fusion.5), channel_id=1, source_target_pairs={{0,128},{1,129},{2,130},{3,131},{4,132},{5,133},{6,134},{7,135},{8... | collective-permute-start | bytes 884744 | tf_op jit(solution)/shard_map/ppermute | solution.py:13
  132.5 11.7 %collective-permute-start.33 = (bf16[2,384,384]{2,1,0:T(8,128)(2,1)S(1)}, bf16[2,384,384]{2,1,0:T(8,128)(2,1)S(1)}, u32[]{:S(2)}, u32[]{:S(2)}) collective-permute-start(bf16[2,384,384]{2,1,0:T(8,128)(2,1)S(1)} %broadcast_select_fusion.1), channel_id=1, source_target_pairs={{0,2},{4,6},{8,10},{12,14},{16,18},{20,22},{24,26},{28,30},{33,35}... | collective-permute-start | bytes 1769480 | tf_op jit(solution)/shard_map/ppermute | solution.py:13
  141.1 17.1 %collective-permute-start.26 = (bf16[2,2,192,384]{3,2,1,0:T(8,128)(2,1)S(1)}, bf16[2,2,192,384]{3,2,1,0:T(8,128)(2,1)S(1)}, u32[]{:S(2)}, u32[]{:S(2)}) collective-permute-start(bf16[2,2,192,384]{3,2,1,0:T(8,128)(2,1)S(1)} %pad_maximum_fusion.2), channel_id=1, source_target_pairs={{0,384},{1,385},{2,386},{3,387},{4,388},{5,389},{6,390},{7,391},{8... | collective-permute-start | bytes 1769480 | tf_op jit(solution)/shard_map/ppermute | solution.py:13
  144.3 15.4 %collective-permute-start.34 = (bf16[2,384,384]{2,1,0:T(8,128)(2,1)S(1)}, bf16[2,384,384]{2,1,0:T(8,128)(2,1)S(1)}, u32[]{:S(2)}, u32[]{:S(2)}) collective-permute-start(bf16[2,384,384]{2,1,0:T(8,128)(2,1)S(1)} %broadcast_select_fusion.2), channel_id=1, source_target_pairs={{0,1},{2,3},{4,5},{6,7},{8,9},{10,11},{12,13},{14,15},{16,17},{18,... | collective-permute-start | bytes 1769480 | tf_op jit(solution)/shard_map/ppermute | solution.py:13
  (30 other events, 194.4 us)
where the time goes:
time: 169 us; the launch traced here: 168 us
  starting transfers between devices  70.6 us (42%)
  waiting for transfers between devices  59.5 us (35%)
  Pallas kernels  21.6 us (13%)
  other arithmetic  8.13 us (5%)
  local copies, waits for them, and re-layouts  7.47 us (4%)
    ppermute x35, starting transfers between devices, send(): return lax.ppermute(x, ('row', 'col'), flat)  70.6 us
    ppermute x35, waiting for transfers between devices, send(): return lax.ppermute(x, ('row', 'col'), flat)  59.5 us
    pallas_call x4, Pallas kernels, run(): pl.pallas_call(kernel, out_shape=outs, in_specs=[pl.BlockSpec(memory_spac...  21.6 us
    unnamed x38, local copies, waits for them, and re-layouts  5.25 us
  transfers between devices with their start and end apart: 35, of which 9 were waited for; matrix products, arithmetic and copies ran while one was open for 5% of the time, Pallas kernels for 6%

commit v1 on v0

--- a/solution.py
+++ b/solution.py
@@ -6,6 +6,7 @@
 from jax.sharding import PartitionSpec as P
 
 ROWS, COLS = 32, 16
+GRANT = {"K2": 12, "K1": 16, "K0": 20, "KF": 28}
 
 
 def send(x, pairs):
@@ -49,8 +50,8 @@
     return chosen.astype(jnp.bfloat16)
 
 
-def first_wave(info, c, u, p, lam, vm, q, x, xb):
-    value = solve(tile_of(c, info[0]), (u, p, lam), (vm, q))
+def first_wave(c, u, p, lam, vm, q, x, xb):
+    value = solve(c[...], (u, p, lam), (vm, q))
     x[...] = value
     xb[...] = value.astype(jnp.bfloat16)
 
@@ -58,7 +59,7 @@
 def second_wave(info, c, n, below, across, own, b_band, u, p, lam, vm, q, x, xb):
     slot = info[1]
     left = either(slot == 0, across[...], own[...])
-    residue = tile_of(c, slot) - dot(tile_of(n, slot), below[...]) - dot(left, tile_of(b_band, slot))
+    residue = c[...] - dot(tile_of(n, slot), below[...]) - dot(left, tile_of(b_band, slot))
     value = solve(residue, (u, p, lam), (vm, q))
     x[...] = value
     xb[...] = value.astype(jnp.bfloat16)
@@ -73,7 +74,7 @@
     left = either(slot == 0, row_one[...], own[...])
     a_tile = either(slot == 0, a[:, tile:], n[:, :tile])
     residue = (
-        tile_of(c, slot)
+        c[...]
         - dot(tile_of(n, slot), col_two[...])
         - dot(row_two[...], tile_of(b_band, slot))
         - dot(a_tile, col_one[...])
@@ -82,55 +83,86 @@
     value = solve(residue, (u, p, lam), (vm, q))
     x[...] = value
     packed = value.astype(jnp.bfloat16)
-    down[0] = col_one[...]
-    down[1] = packed
-    across[0] = left
-    across[1] = packed
+    down[0] = packed
+    down[1] = col_one[...]
+    down[2] = col_two[...]
+    across[0] = packed
+    across[1] = left
+    across[2] = row_two[...]
 
 
 def last_update(
-    info, c, a, n, b, b_above, b_above_two, down_two, down, row_two, across, x_two, x_one, x_zero, out
+    info, c, a, n, b, b_above, b_above_two, p_one, p_two, q_one, q_two, across, flipped,
+    x_two, x_one, x_zero, out, down,
 ):
     tile = c.shape[0]
+    piece = p_one.shape[-2]
     a_tiles = (a.at[:, :tile], a.at[:, tile:], n.at[:, :tile], n.at[:, tile:])
+    b_tiles = (b, b_above, b_above_two)
+    where = info[3]
+
+    @pl.when(where < 1)
+    def _():
+        for wave in range(3):
+            for member in range(2):
+                index = member ^ info[4]
+                for start, (first, second) in ((0, (p_one, p_two)), (piece, (q_one, q_two))):
+                    near = 5 if start == 0 else 9
+                    for slot in range(2):
+                        at = pl.ds(pl.multiple_of(info[near + slot] * 2 * piece + start, 16), piece)
+                        down[member, wave, at, :] = first[slot, index, wave]
+                        at = pl.ds(
+                            pl.multiple_of(info[near + 2 + slot] * 2 * piece + start, 16), piece
+                        )
+                        down[member, wave, at, :] = second[slot, index, wave]
+
+    def update(member, source):
+        span = slice(member * tile, (member + 1) * tile)
+        change = dot(a_tiles[member][...], down[member, 0])
+        for wave in (1, 2):
+            change += dot(a_tiles[member + wave][...], down[member, wave])
+        for wave in range(3):
+            change += dot(source[wave], b_tiles[wave][:, span])
+        out[:, span] = c[:, span] - change
+
     for member in range(2):
-        where = info[3] - member
         span = slice(member * tile, (member + 1) * tile)
 
-        @pl.when(where < 0)
+        @pl.when((where < member) & (info[13] == 0))
         def _():
-            change = dot(a_tiles[member][...], down[member, 1])
-            change += dot(a_tiles[member + 1][...], down[member, 0])
-            change += dot(a_tiles[member + 2][...], down_two[member, 0])
-            change += dot(across[1], b[:, span])
-            change += dot(across[0], b_above[:, span])
-            change += dot(row_two[0], b_above_two[:, span])
-            out[:, span] = c[:, span] - change
+            update(member, across)
+
+        @pl.when((where < member) & (info[13] == 1))
+        def _():
+            update(member, flipped)
 
         for wave, solved in enumerate((x_zero, x_one, x_two)):
 
-            @pl.when(where == wave)
+            @pl.when(where == wave + member)
             def _():
                 out[:, span] = solved[...]
 
-        @pl.when(where > 2)
+        @pl.when(where > 2 + member)
         def _():
             out[:, span] = c[:, span]
 
 
-def run(kernel, outs, dots, info, *operands):
+def run(name, kernel, outs, dots, info, *operands, scratch=()):
     tile = operands[0].shape[0]
     moved = sum(v.size * v.dtype.itemsize for v in (*operands, *outs))
     whole = pl.BlockSpec(memory_space=pltpu.VMEM)
+    scalars = () if info is None else (info,)
     return pl.pallas_call(
         kernel,
         out_shape=outs,
-        in_specs=[pl.BlockSpec(memory_space=pltpu.SMEM)] + [whole] * len(operands),
+        in_specs=[pl.BlockSpec(memory_space=pltpu.SMEM)] * len(scalars) + [whole] * len(operands),
         out_specs=[whole] * len(outs),
+        scratch_shapes=scratch,
+        compiler_params=pltpu.CompilerParams(vmem_limit_bytes=GRANT[name] << 20),
         cost_estimate=pl.CostEstimate(
             flops=2 * dots * tile**3, bytes_accessed=moved, transcendentals=0
         ),
-    )(info, *operands)
+    )(*scalars, *operands)
 
 
 def row_tree(x, offset):
@@ -151,7 +183,7 @@
             if (c ^ 1) > k // 2:
                 pairs.append(((k, c), (k, c ^ 1)))
     got = send(x, pairs)
-    return jnp.where(offset % 2 == 0, x, got)
+    return x, got
 
 
 def col_spread(x, row, col):
@@ -169,7 +201,6 @@
     got = send(part[:, quarter:], pairs)
     first = (relative == 0) | (relative == 3)
     part = jnp.where(first, part[:, :quarter], got)
-    source = (col % 4) // 2
     base = 2 * (col % 4)
     pairs = [((q * 8 + s, c), (q * 8 + 7 - s, c)) for _, s, c in diagonal for q in range(4)]
     got = send(part, pairs)
@@ -184,13 +215,15 @@
     part = jnp.where(holds, part, got)
     every = [(r, c) for r in range(ROWS) for c in range(COLS)]
     got = send(part, [((r, c), (r ^ 1, c)) for r, c in every])
-    is_second = (z % 2) ^ ((z // 4) != source).astype(jnp.int32)
-    both = jnp.stack([jnp.where(is_second == 0, part, got), jnp.where(is_second == 0, got, part)])
-    got = send(both, [((r, c), (r ^ 8, c)) for r, c in every])
-    both = jnp.concatenate([jnp.where(first, both, got), jnp.where(first, got, both)], axis=2)
-    got = send(both, [((r, c), (r ^ 24, c)) for r, c in every])
-    upper = relative <= 1
-    return jnp.concatenate([jnp.where(upper, both, got), jnp.where(upper, got, both)], axis=2)
+    both = jnp.stack([part, got])
+    near = [((r, c), (r ^ 8, c)) for r, c in every]
+    far = [((r, c), (r ^ 24, c)) for r, c in every]
+    piece = tile // 8
+    p_one = both[:, :, :piece]
+    q_one = both[:, :, piece:]
+    p_one = jnp.stack([p_one, send(p_one, near)])
+    q_one = jnp.stack([q_one, send(q_one, far)])
+    return p_one, send(p_one, far), q_one, send(q_one, near)
 
 
 def shards(
@@ -200,11 +233,22 @@
     row = lax.axis_index("row")
     col = lax.axis_index("col")
     d = row - 2 * col
-    info = jnp.stack([jnp.clip(d - 2, 0, 1), jnp.clip(d - 1, 0, 1), jnp.clip(d, 0, 1), d])
+    relative = (row // 8) ^ (col // 4)
+    z = row % 8
+    flips = [relative ^ flip for flip in (0, 1, 3, 2, 0, 3, 1, 2)]
+    order = [plane ^ (plane // 2) for plane in flips]
+    swapped = (z % 2) ^ ((z // 4) != (col % 4) // 2).astype(jnp.int32)
+    parity = jnp.abs(col - row // 2) % 2
+    slots = [jnp.clip(d - wave, 0, 1) for wave in (2, 1, 0)]
+    info = jnp.stack([*slots, d, swapped, *order, parity])
+    c_two, c_one, c_zero = (
+        lax.dynamic_slice_in_dim(c_matrix, slot * a_vectors.shape[1], a_vectors.shape[1], 1)
+        for slot in slots
+    )
     left = (a_vectors, a_inverse, a_values.astype(jnp.float32)[:, None])
     square = jax.ShapeDtypeStruct((tile, tile), jnp.bfloat16)
     exact = jax.ShapeDtypeStruct((tile, tile), jnp.float32)
-    pair = jax.ShapeDtypeStruct((2, tile, tile), jnp.bfloat16)
+    three = jax.ShapeDtypeStruct((3, tile, tile), jnp.bfloat16)
 
     packed = jnp.concatenate([b_vectors, jnp.broadcast_to(b_values[None], (16, tile))])
     packed_one = send(packed, band((0, 1), 1, 0))
@@ -221,30 +265,32 @@
     b_above = send(b_upper, rows_down(1))
     b_above_two = send(b_above, rows_down(0))
 
-    x_two, solved_two = run(first_wave, (exact, square), 4, info, c_matrix, *left, packed_two, inverse_two)
+    x_two, solved_two = run(
+        "K2", first_wave, (exact, square), 4, None,
+        c_two.astype(jnp.bfloat16), *left, packed_two, inverse_two,
+    )
     below = send(solved_two, band((2, 3), -1, 0))
     row_two = send(solved_two, band((2, 3), 0, 1))
     col_two = send(solved_two, band((2, 3), -2, 0))
     x_one, solved_one = run(
-        second_wave, (exact, square), 6, info,
-        c_matrix, a_next, below, row_two, solved_two, b_band, *left, packed_one, inverse_one,
+        "K1", second_wave, (exact, square), 6, info,
+        c_one, a_next, below, row_two, solved_two, b_band, *left, packed_one, inverse_one,
     )
     col_one = send(solved_one, band((1, 2), -1, 0))
     row_one = send(solved_one, band((2,), 0, 1))
     x_zero, down, across = run(
-        third_wave, (exact, pair, pair), 8, info,
-        c_matrix, a_upper, a_next, col_two, row_two, col_one, row_one, solved_one,
+        "K0", third_wave, (exact, three, three), 8, info,
+        c_zero, a_upper, a_next, col_two, row_two, col_one, row_one, solved_one,
         b_band, b_above, *left, packed, b_inverse,
     )
     offset = col - row // 2
-    down_two = col_spread(col_two[None], row, col)
-    across_two = row_tree(row_two[None], offset)
-    down = col_spread(down, row, col)
-    across = row_tree(across, offset)
+    pieces = col_spread(down, row, col)
+    across, flipped = row_tree(across, offset)
     return run(
-        last_update, (jax.ShapeDtypeStruct(c_matrix.shape, jnp.float32),), 12, info,
+        "KF", last_update, (jax.ShapeDtypeStruct(c_matrix.shape, jnp.float32),), 12, info,
         c_matrix, a_upper, a_next, b_upper, b_above, b_above_two,
-        down_two, down, across_two, across, x_two, x_one, x_zero,
+        *pieces, across, flipped, x_two, x_one, x_zero,
+        scratch=[pltpu.VMEM((2, 3, tile, tile), jnp.bfloat16)],
     )[0]
 
 
@@ -261,4 +307,6 @@
         P("row"),
     )
 
-    return jax.shard_map(shards, mesh=mesh, in_specs=placed, out_specs=P("row", "col"), check_vma=False)
+    return jax.shard_map(
+        shards, mesh=mesh, in_specs=placed, out_specs=P("row", "col"), check_vma=False
+    )

time: 169 us -> 165 us (0.976)
  the two profiles are of different devices: /device:TPU:152 before, /device:TPU:62 now
where the time goes in v1:
time: 165 us; the launch traced here: 164 us
  waiting for transfers between devices  80.2 us (49%)
  starting transfers between devices  54.1 us (33%)
  Pallas kernels  15.4 us (9%)
  local copies, waits for them, and re-layouts  7.33 us (4%)
  other arithmetic  6.11 us (4%)
    ppermute x26, waiting for transfers between devices, send(): return lax.ppermute(x, ('row', 'col'), flat)  80.2 us
    ppermute x26, starting transfers between devices, send(): return lax.ppermute(x, ('row', 'col'), flat)  54.1 us
    pallas_call x4, Pallas kernels, run(): pl.pallas_call(kernel, out_shape=outs, in_specs=[pl.BlockSpec(memory_spac...  15.4 us
    select_n x3, other arithmetic, row_tree(): x = jnp.where(takes, got, x)  4.82 us
    unnamed x28, local copies, waits for them, and re-layouts  3.44 us
  transfers between devices with their start and end apart: 26, of which 6 were waited for; matrix products, arithmetic and copies ran while one was open for 5% of the time, Pallas kernels for 4%

profile of v1, /device:TPU:62, one launch (start us, length us, event | category | flops | bytes accessed | tf_op | source)
XLA Modules:
  0.0 164.0 jit_solution(8036124511097755227)
XLA Ops:
  1.7 1.4 collective-permute-start.3
  7.3 2.7 %collective-permute-start = (bf16[384,768]{1,0:T(8,128)(2,1)}, bf16[384,768]{1,0:T(8,128)(2,1)S(1)}, u32[]{:S(2)}, u32[]{:S(2)}) collective-permute-start(bf16[384,768]{1,0:T(8,128)(2,1)} %a.3), channel_id=1, source_target_pairs={{1,0},{2,1},{3,2},{4,3},{5,4},{6,5},{7,6},{8,7},{9,8},{10,9},{11,1... | collective-permute-start | bytes 1769480 | tf_op jit(solution)/shard_map/ppermute | solution.py:14
  12.7 3.0 %shard_map.91 = (f32[384,384]{1,0:T(8,128)S(1)}, bf16[384,384]{1,0:T(8,128)(2,1)}) custom-call(bf16[384,384]{1,0:T(8,128)(2,1)S(1)} %dynamic-slice_convert_fusion.c, bf16[384,384]{1,0:T(8,128)(2,1)S(1)} %copy-done.1, bf16[384,384]{1,0:T(8,128)(2,1)S(1)} %copy-done.2, f32[384,1]{1,0:T(8,128)S(1)} %reshape.2.lam, bf16[400,384]{1,0:T(8,128)(2,1)} %collective-permute-done.4.vm, ...), custom_call_target="tpu_custom_call" | custom-call | flops 452984832 | bytes 2373120 | tf_op jit(solution)/shard_map/pallas_call | solution.py:155
  19.3 4.3 %collective-permute-start.1 = (bf16[384,768]{1,0:T(8,128)(2,1)}, bf16[384,768]{1,0:T(8,128)(2,1)}, u32[]{:S(2)}, u32[]{:S(2)}) collective-permute-start(bf16[384,768]{1,0:T(8,128)(2,1)} %b.1), channel_id=1, source_target_pairs={{0,16},{1,17},{2,18},{3,19},{4,20},{5,21},{6,22},{7,23},{8,24},{9,... | collective-permute-start | bytes 1769480 | tf_op jit(solution)/shard_map/ppermute | solution.py:14
  24.7 3.0 %shard_map.92 = (f32[384,384]{1,0:T(8,128)S(1)}, bf16[384,384]{1,0:T(8,128)(2,1)S(1)}) custom-call(s32[14]{0:T(128)S(1)} %stack.74.info, f32[384,384]{1,0:T(8,128)S(1)} %get-tuple-element.19.c, bf16[384,768]{1,0:T(8,128)(2,1)S(1)} %collective-permute-done.n, bf16[384,384]{1,0:T(8,128)(2,1)} %collective-permute-done.9.below, ...), custom_call_target="tpu_custom_call" | custom-call | flops 679477248 | bytes 4732416 | tf_op jit(solution)/shard_map/pallas_call | solution.py:155
  29.9 14.1 %collective-permute-done.1.b_above = bf16[384,768]{1,0:T(8,128)(2,1)} collective-permute-done((bf16[384,768]{1,0:T(8,128)(2,1)}, bf16[384,768]{1,0:T(8,128)(2,1)}, u32[]{:S(2)}, u32[]{:S(2)}) %collective-permute-start.1) | collective-permute-done | bytes 589856 | tf_op jit(solution)/shard_map/ppermute | solution.py:14
  44.1 4.2 %shard_map.93 = (f32[384,384]{1,0:T(8,128)S(1)}, bf16[3,384,384]{2,1,0:T(8,128)(2,1)S(1)}, bf16[3,384,384]{2,1,0:T(8,128)(2,1)}) custom-call(s32[14]{0:T(128)S(1)} %stack.74.info, f32[384,384]{1,0:T(8,128)S(1)} %get-tuple-element.20.c, bf16[384,768]{1,0:T(8,128)(2,1)S(1)} %copy-done.3, bf16[384,768]{1,0:T(8,128)(2,1)S(1)} %collective-permute-done.n, ...), custom_call_target="tpu_custom_call" | custom-call | flops 905969664 | bytes 7976448 | tf_op jit(solution)/shard_map/pallas_call | solution.py:155
  50.0 1.6 collective-permute-start.22
  52.6 1.6 collective-permute-start.13
  54.2 2.2 %broadcast_select_fusion = bf16[3,384,384]{2,1,0:T(8,128)(2,1)} fusion(bf16[3,384,384]{2,1,0:T(8,128)(2,1)} %collective-permute-done.22, bf16[3,384,384]{2,1,0:T(8,128)(2,1)} %get-tuple-element.15, pred[]{:T(512)S(6)} %and.127), kind=kLoop, calls=%fused_computation | loop fusion | flops 442368 | bytes 2654209 | tf_op jit(solution)/shard_map/jit(_where)/select_n | solution.py:179
  56.4 1.6 collective-permute-start.23
  63.6 36.5 %collective-permute-done.16 = bf16[3,96,384]{2,1,0:T(8,128)(2,1)S(1)} collective-permute-done((bf16[3,96,384]{2,1,0:T(8,128)(2,1)S(1)}, bf16[3,96,384]{2,1,0:T(8,128)(2,1)S(1)}, u32[]{:S(2)}, u32[]{:S(2)}) %collective-permute-start.16) | collective-permute-done | bytes 221216 | tf_op jit(solution)/shard_map/ppermute | solution.py:14
  100.1 1.9 %collective-permute-start.17 = (bf16[3,96,384]{2,1,0:T(8,128)(2,1)S(1)}, bf16[3,96,384]{2,1,0:T(8,128)(2,1)S(1)}, u32[]{:S(2)}, u32[]{:S(2)}) collective-permute-start(bf16[3,96,384]{2,1,0:T(8,128)(2,1)S(1)} %broadcast_select_fusion.4), channel_id=1, source_target_pairs={{0,16},{1,17},{2,18},{3,19},{4,20},{5,21},{6,22},{7,23},{8,24},{9,... | collective-permute-start | bytes 663560 | tf_op jit(solution)/shard_map/ppermute | solution.py:14
  102.1 5.9 %collective-permute-done.17 = bf16[3,96,384]{2,1,0:T(8,128)(2,1)S(1)} collective-permute-done((bf16[3,96,384]{2,1,0:T(8,128)(2,1)S(1)}, bf16[3,96,384]{2,1,0:T(8,128)(2,1)S(1)}, u32[]{:S(2)}, u32[]{:S(2)}) %collective-permute-start.17) | collective-permute-done | bytes 221216 | tf_op jit(solution)/shard_map/ppermute | solution.py:14
  108.0 14.3 %collective-permute-start.20 = (bf16[2,3,48,384]{3,2,1,0:T(8,128)(2,1)S(1)}, bf16[2,3,48,384]{3,2,1,0:T(8,128)(2,1)S(1)}, u32[]{:S(2)}, u32[]{:S(2)}) collective-permute-start(bf16[2,3,48,384]{3,2,1,0:T(8,128)(2,1)S(1)} %get-tuple-element.21), channel_id=1, source_target_pairs={{0,384},{1,385},{2,386},{3,387},{4,388},{5,389},{6,390},{7,391},{8... | collective-permute-start | bytes 663560 | tf_op jit(solution)/shard_map/ppermute | solution.py:14
  123.8 1.5 collective-permute-start.25
  125.2 3.7 %collective-permute-start.18 = (bf16[2,3,48,384]{3,2,1,0:T(8,128)(2,1)S(1)}, bf16[2,3,48,384]{3,2,1,0:T(8,128)(2,1)S(1)}, u32[]{:S(2)}, u32[]{:S(2)}) collective-permute-start(bf16[2,3,48,384]{3,2,1,0:T(8,128)(2,1)S(1)} %get-tuple-element.22), channel_id=1, source_target_pairs={{0,128},{1,129},{2,130},{3,131},{4,132},{5,133},{6,134},{7,135},{8... | collective-permute-start | bytes 663560 | tf_op jit(solution)/shard_map/ppermute | solution.py:14
  128.9 1.9 %collective-permute-start.2 = (bf16[384,768]{1,0:T(8,128)(2,1)}, bf16[384,768]{1,0:T(8,128)(2,1)S(1)}, u32[]{:S(2)}, u32[]{:S(2)}) collective-permute-start(bf16[384,768]{1,0:T(8,128)(2,1)} %collective-permute-done.1.b_above), channel_id=1, source_target_pairs={{1,17},{2,18},{3,19},{4,20},{5,21},{6,22},{7,23},{8,24},{9,25},{10... | collective-permute-start | bytes 1769480 | tf_op jit(solution)/shard_map/ppermute | solution.py:14
  130.9 2.2 %collective-permute-start.21 = (bf16[2,2,3,48,384]{4,3,2,1,0:T(8,128)(2,1)S(1)}, bf16[2,2,3,48,384]{4,3,2,1,0:T(8,128)(2,1)S(1)}, u32[]{:S(2)}, u32[]{:S(2)}) collective-permute-start(bf16[2,2,3,48,384]{4,3,2,1,0:T(8,128)(2,1)S(1)} %pad_maximum_fusion.1.q_one), channel_id=1, source_target_pairs={{0,128},{1,129},{2,130},{3,131},{4,132},{5,133},{6,134},{7,135},{8... | collective-permute-start | bytes 1327112 | tf_op jit(solution)/shard_map/ppermute | solution.py:14
  133.1 14.2 %collective-permute-done.18 = bf16[2,3,48,384]{3,2,1,0:T(8,128)(2,1)S(1)} collective-permute-done((bf16[2,3,48,384]{3,2,1,0:T(8,128)(2,1)S(1)}, bf16[2,3,48,384]{3,2,1,0:T(8,128)(2,1)S(1)}, u32[]{:S(2)}, u32[]{:S(2)}) %collective-permute-start.18) | collective-permute-done | bytes 221216 | tf_op jit(solution)/shard_map/ppermute | solution.py:14
  147.3 1.9 %collective-permute-start.19 = (bf16[2,2,3,48,384]{4,3,2,1,0:T(8,128)(2,1)S(1)}, bf16[2,2,3,48,384]{4,3,2,1,0:T(8,128)(2,1)S(1)}, u32[]{:S(2)}, u32[]{:S(2)}) collective-permute-start(bf16[2,2,3,48,384]{4,3,2,1,0:T(8,128)(2,1)S(1)} %pad_maximum_fusion.p_one), channel_id=1, source_target_pairs={{0,384},{1,385},{2,386},{3,387},{4,388},{5,389},{6,390},{7,391},{8... | collective-permute-start | bytes 1327112 | tf_op jit(solution)/shard_map/ppermute | solution.py:14
  149.3 2.7 %collective-permute-done.21.q_two = bf16[2,2,3,48,384]{4,3,2,1,0:T(8,128)(2,1)S(1)} collective-permute-done((bf16[2,2,3,48,384]{4,3,2,1,0:T(8,128)(2,1)S(1)}, bf16[2,2,3,48,384]{4,3,2,1,0:T(8,128)(2,1)S(1)}, u32[]{:S(2)}, u32[]{:S(2)}) %collective-permute-start.21) | collective-permute-done | bytes 442400 | tf_op jit(solution)/shard_map/ppermute | solution.py:14
  152.0 6.7 %collective-permute-done.19.p_two = bf16[2,2,3,48,384]{4,3,2,1,0:T(8,128)(2,1)S(1)} collective-permute-done((bf16[2,2,3,48,384]{4,3,2,1,0:T(8,128)(2,1)S(1)}, bf16[2,2,3,48,384]{4,3,2,1,0:T(8,128)(2,1)S(1)}, u32[]{:S(2)}, u32[]{:S(2)}) %collective-permute-start.19) | collective-permute-done | bytes 442400 | tf_op jit(solution)/shard_map/ppermute | solution.py:14
  158.8 5.2 %shard_map.94 = f32[384,768]{1,0:T(8,128)} custom-call(s32[14]{0:T(128)S(1)} %stack.74.info, f32[384,768]{1,0:T(8,128)S(1)} %copy-done, bf16[384,768]{1,0:T(8,128)(2,1)S(1)} %copy-done.4, bf16[384,768]{1,0:T(8,128)(2,1)S(1)} %collective-permute-done.n, bf16[384,768]{1,0:T(8,128)(2,1)} %b.1, bf16[384,768]{1,0:T(8,128)(2,1)} %collective-permute-done.1.b_above, ...), custom_call_target="tpu_custom_call" | custom-call | flops 1358954496 | bytes 10616832 | tf_op jit(solution)/shard_map/pallas_call | solution.py:155
  (78 shorter events, 24.9 us)
Async XLA Ops:
  3.1 2.8 %collective-permute-start.5 = (bf16[384,384]{1,0:T(8,128)(2,1)}, bf16[384,384]{1,0:T(8,128)(2,1)}, u32[]{:S(2)}, u32[]{:S(2)}) collective-permute-start(bf16[384,384]{1,0:T(8,128)(2,1)} %q.1), channel_id=1, source_target_pairs={{0,16},{16,32},{33,49},{49,65},{66,82},{82,98},{99,115},{115,131},... | collective-permute-start | bytes 884744 | tf_op jit(solution)/shard_map/ppermute | solution.py:14
  4.5 8.1 %collective-permute-start.4 = (bf16[400,384]{1,0:T(8,128)(2,1)}, bf16[400,384]{1,0:T(8,128)(2,1)}, u32[]{:S(2)}, u32[]{:S(2)}) collective-permute-start(bf16[400,384]{1,0:T(8,128)(2,1)} %collective-permute-done.3.vm), channel_id=1, source_target_pairs={{16,32},{32,48},{49,65},{65,81},{82,98},{98,114},{115,131},{131,14... | collective-permute-start | bytes 921608 | tf_op jit(solution)/shard_map/ppermute | solution.py:14
  5.9 6.7 %collective-permute-start.6 = (bf16[384,384]{1,0:T(8,128)(2,1)}, bf16[384,384]{1,0:T(8,128)(2,1)}, u32[]{:S(2)}, u32[]{:S(2)}) collective-permute-start(bf16[384,384]{1,0:T(8,128)(2,1)} %collective-permute-done.5.q), channel_id=1, source_target_pairs={{16,32},{32,48},{49,65},{65,81},{82,98},{98,114},{115,131},{131,14... | collective-permute-start | bytes 884744 | tf_op jit(solution)/shard_map/ppermute | solution.py:14
  7.3 16.7 %collective-permute-start = (bf16[384,768]{1,0:T(8,128)(2,1)}, bf16[384,768]{1,0:T(8,128)(2,1)S(1)}, u32[]{:S(2)}, u32[]{:S(2)}) collective-permute-start(bf16[384,768]{1,0:T(8,128)(2,1)} %a.3), channel_id=1, source_target_pairs={{1,0},{2,1},{3,2},{4,3},{5,4},{6,5},{7,6},{8,7},{9,8},{10,9},{11,1... | collective-permute-start | bytes 1769480 | tf_op jit(solution)/shard_map/ppermute | solution.py:14
  10.0 14.7 %collective-permute-start.10 = (bf16[384,768]{1,0:T(8,128)(2,1)}, bf16[384,768]{1,0:T(8,128)(2,1)S(1)}, u32[]{:S(2)}, u32[]{:S(2)}) collective-permute-start(bf16[384,768]{1,0:T(8,128)(2,1)} %b.1), channel_id=1, source_target_pairs={{0,32},{1,33},{17,49},{33,65},{34,66},{50,82},{66,98},{67,99},{83,... | collective-permute-start | bytes 1769480 | tf_op jit(solution)/shard_map/ppermute | solution.py:14
  16.5 8.2 %collective-permute-start.8 = (bf16[384,384]{1,0:T(8,128)(2,1)}, bf16[384,384]{1,0:T(8,128)(2,1)}, u32[]{:S(2)}, u32[]{:S(2)}) collective-permute-start(bf16[384,384]{1,0:T(8,128)(2,1)} %get-tuple-element.12.own), channel_id=1, source_target_pairs={{32,33},{48,49},{65,66},{81,82},{98,99},{114,115},{131,132},{147,1... | collective-permute-start | bytes 884744 | tf_op jit(solution)/shard_map/ppermute | solution.py:14
  17.9 6.8 %collective-permute-start.9 = (bf16[384,384]{1,0:T(8,128)(2,1)}, bf16[384,384]{1,0:T(8,128)(2,1)}, u32[]{:S(2)}, u32[]{:S(2)}) collective-permute-start(bf16[384,384]{1,0:T(8,128)(2,1)} %get-tuple-element.12.own), channel_id=1, source_target_pairs={{32,16},{48,32},{65,49},{81,65},{98,82},{114,98},{131,115},{147,13... | collective-permute-start | bytes 884744 | tf_op jit(solution)/shard_map/ppermute | solution.py:14
  19.3 24.8 %collective-permute-start.1 = (bf16[384,768]{1,0:T(8,128)(2,1)}, bf16[384,768]{1,0:T(8,128)(2,1)}, u32[]{:S(2)}, u32[]{:S(2)}) collective-permute-start(bf16[384,768]{1,0:T(8,128)(2,1)} %b.1), channel_id=1, source_target_pairs={{0,16},{1,17},{2,18},{3,19},{4,20},{5,21},{6,22},{7,23},{8,24},{9,... | collective-permute-start | bytes 1769480 | tf_op jit(solution)/shard_map/ppermute | solution.py:14
  24.0 20.0 %collective-permute-start.7 = (bf16[384,384]{1,0:T(8,128)(2,1)}, bf16[384,384]{1,0:T(8,128)(2,1)S(1)}, u32[]{:S(2)}, u32[]{:S(2)}) collective-permute-start(bf16[384,384]{1,0:T(8,128)(2,1)} %get-tuple-element.12.own), channel_id=1, source_target_pairs={{32,0},{48,16},{65,33},{81,49},{98,66},{114,82},{131,99},{147,115}... | collective-permute-start | bytes 884744 | tf_op jit(solution)/shard_map/ppermute | solution.py:14
  28.6 15.5 %collective-permute-start.11 = (bf16[384,384]{1,0:T(8,128)(2,1)S(1)}, bf16[384,384]{1,0:T(8,128)(2,1)S(1)}, u32[]{:S(2)}, u32[]{:S(2)}) collective-permute-start(bf16[384,384]{1,0:T(8,128)(2,1)S(1)} %get-tuple-element.13.own), channel_id=1, source_target_pairs={{16,0},{32,16},{49,33},{65,49},{82,66},{98,82},{115,99},{131,115},... | collective-permute-start | bytes 884744 | tf_op jit(solution)/shard_map/ppermute | solution.py:14
  29.3 14.8 %collective-permute-start.12 = (bf16[384,384]{1,0:T(8,128)(2,1)S(1)}, bf16[384,384]{1,0:T(8,128)(2,1)S(1)}, u32[]{:S(2)}, u32[]{:S(2)}) collective-permute-start(bf16[384,384]{1,0:T(8,128)(2,1)S(1)} %get-tuple-element.13.own), channel_id=1, source_target_pairs={{32,33},{65,66},{98,99},{131,132},{164,165},{197,198},{230,231},{2... | collective-permute-start | bytes 884744 | tf_op jit(solution)/shard_map/ppermute | solution.py:14
  50.0 4.2 %collective-permute-start.22 = (bf16[3,384,384]{2,1,0:T(8,128)(2,1)}, bf16[3,384,384]{2,1,0:T(8,128)(2,1)}, u32[]{:S(2)}, u32[]{:S(2)}) collective-permute-start(bf16[3,384,384]{2,1,0:T(8,128)(2,1)} %get-tuple-element.15), channel_id=1, source_target_pairs={{0,8},{16,24},{33,41},{49,57},{66,74},{82,90},{99,107},{115,123},{... | collective-permute-start | bytes 2654216 | tf_op jit(solution)/shard_map/ppermute | solution.py:14
  52.6 5.4 %collective-permute-start.13 = (bf16[3,192,384]{2,1,0:T(8,128)(2,1)S(1)}, bf16[3,192,384]{2,1,0:T(8,128)(2,1)}, u32[]{:S(2)}, u32[]{:S(2)}) collective-permute-start(bf16[3,192,384]{2,1,0:T(8,128)(2,1)S(1)} %slice.19), channel_id=1, source_target_pairs={{0,384},{16,400},{33,417},{49,433},{66,450},{82,466},{99,483},{115... | collective-permute-start | bytes 1327112 | tf_op jit(solution)/shard_map/ppermute | solution.py:14
  56.4 3.1 %collective-permute-start.23 = (bf16[3,384,384]{2,1,0:T(8,128)(2,1)}, bf16[3,384,384]{2,1,0:T(8,128)(2,1)}, u32[]{:S(2)}, u32[]{:S(2)}) collective-permute-start(bf16[3,384,384]{2,1,0:T(8,128)(2,1)} %broadcast_select_fusion), channel_id=1, source_target_pairs={{0,4},{8,12},{16,20},{24,28},{33,37},{41,45},{49,53},{57,61},{66,7... | collective-permute-start | bytes 2654216 | tf_op jit(solution)/shard_map/ppermute | solution.py:14
  58.9 3.3 %collective-permute-start.15 = (bf16[3,96,384]{2,1,0:T(8,128)(2,1)S(1)}, bf16[3,96,384]{2,1,0:T(8,128)(2,1)S(1)}, u32[]{:S(2)}, u32[]{:S(2)}) collective-permute-start(bf16[3,96,384]{2,1,0:T(8,128)(2,1)S(1)} %slice_select_fusion.1), channel_id=1, source_target_pairs={{0,112},{128,240},{256,368},{384,496},{16,96},{144,224},{272,352},... | collective-permute-start | bytes 663560 | tf_op jit(solution)/shard_map/ppermute | solution.py:14
  60.9 61.5 %collective-permute-start.24 = (bf16[3,384,384]{2,1,0:T(8,128)(2,1)S(1)}, bf16[3,384,384]{2,1,0:T(8,128)(2,1)}, u32[]{:S(2)}, u32[]{:S(2)}) collective-permute-start(bf16[3,384,384]{2,1,0:T(8,128)(2,1)S(1)} %broadcast_select_fusion.1), channel_id=1, source_target_pairs={{0,2},{4,6},{8,10},{12,14},{16,18},{20,22},{24,26},{28,30},{33,35}... | collective-permute-start | bytes 2654216 | tf_op jit(solution)/shard_map/ppermute | solution.py:14
  62.2 37.9 %collective-permute-start.16 = (bf16[3,96,384]{2,1,0:T(8,128)(2,1)S(1)}, bf16[3,96,384]{2,1,0:T(8,128)(2,1)S(1)}, u32[]{:S(2)}, u32[]{:S(2)}) collective-permute-start(bf16[3,96,384]{2,1,0:T(8,128)(2,1)S(1)} %broadcast_select_fusion.3), channel_id=1, source_target_pairs={{0,32},{112,80},{128,160},{240,208},{256,288},{368,336},{384,416},... | collective-permute-start | bytes 663560 | tf_op jit(solution)/shard_map/ppermute | solution.py:14
  100.1 7.8 %collective-permute-start.17 = (bf16[3,96,384]{2,1,0:T(8,128)(2,1)S(1)}, bf16[3,96,384]{2,1,0:T(8,128)(2,1)S(1)}, u32[]{:S(2)}, u32[]{:S(2)}) collective-permute-start(bf16[3,96,384]{2,1,0:T(8,128)(2,1)S(1)} %broadcast_select_fusion.4), channel_id=1, source_target_pairs={{0,16},{1,17},{2,18},{3,19},{4,20},{5,21},{6,22},{7,23},{8,24},{9,... | collective-permute-start | bytes 663560 | tf_op jit(solution)/shard_map/ppermute | solution.py:14
  108.0 22.8 %collective-permute-start.20 = (bf16[2,3,48,384]{3,2,1,0:T(8,128)(2,1)S(1)}, bf16[2,3,48,384]{3,2,1,0:T(8,128)(2,1)S(1)}, u32[]{:S(2)}, u32[]{:S(2)}) collective-permute-start(bf16[2,3,48,384]{3,2,1,0:T(8,128)(2,1)S(1)} %get-tuple-element.21), channel_id=1, source_target_pairs={{0,384},{1,385},{2,386},{3,387},{4,388},{5,389},{6,390},{7,391},{8... | collective-permute-start | bytes 663560 | tf_op jit(solution)/shard_map/ppermute | solution.py:14
  123.8 35.0 %collective-permute-start.25 = (bf16[3,384,384]{2,1,0:T(8,128)(2,1)S(1)}, bf16[3,384,384]{2,1,0:T(8,128)(2,1)S(1)}, u32[]{:S(2)}, u32[]{:S(2)}) collective-permute-start(bf16[3,384,384]{2,1,0:T(8,128)(2,1)S(1)} %broadcast_select_fusion.2.across), channel_id=1, source_target_pairs={{0,1},{2,3},{4,5},{6,7},{8,9},{10,11},{12,13},{14,15},{16,17},{18,... | collective-permute-start | bytes 2654216 | tf_op jit(solution)/shard_map/ppermute | solution.py:14
  125.2 22.0 %collective-permute-start.18 = (bf16[2,3,48,384]{3,2,1,0:T(8,128)(2,1)S(1)}, bf16[2,3,48,384]{3,2,1,0:T(8,128)(2,1)S(1)}, u32[]{:S(2)}, u32[]{:S(2)}) collective-permute-start(bf16[2,3,48,384]{3,2,1,0:T(8,128)(2,1)S(1)} %get-tuple-element.22), channel_id=1, source_target_pairs={{0,128},{1,129},{2,130},{3,131},{4,132},{5,133},{6,134},{7,135},{8... | collective-permute-start | bytes 663560 | tf_op jit(solution)/shard_map/ppermute | solution.py:14
  128.9 20.3 %collective-permute-start.2 = (bf16[384,768]{1,0:T(8,128)(2,1)}, bf16[384,768]{1,0:T(8,128)(2,1)S(1)}, u32[]{:S(2)}, u32[]{:S(2)}) collective-permute-start(bf16[384,768]{1,0:T(8,128)(2,1)} %collective-permute-done.1.b_above), channel_id=1, source_target_pairs={{1,17},{2,18},{3,19},{4,20},{5,21},{6,22},{7,23},{8,24},{9,25},{10... | collective-permute-start | bytes 1769480 | tf_op jit(solution)/shard_map/ppermute | solution.py:14
  130.9 21.1 %collective-permute-start.21 = (bf16[2,2,3,48,384]{4,3,2,1,0:T(8,128)(2,1)S(1)}, bf16[2,2,3,48,384]{4,3,2,1,0:T(8,128)(2,1)S(1)}, u32[]{:S(2)}, u32[]{:S(2)}) collective-permute-start(bf16[2,2,3,48,384]{4,3,2,1,0:T(8,128)(2,1)S(1)} %pad_maximum_fusion.1.q_one), channel_id=1, source_target_pairs={{0,128},{1,129},{2,130},{3,131},{4,132},{5,133},{6,134},{7,135},{8... | collective-permute-start | bytes 1327112 | tf_op jit(solution)/shard_map/ppermute | solution.py:14
  147.3 11.4 %collective-permute-start.19 = (bf16[2,2,3,48,384]{4,3,2,1,0:T(8,128)(2,1)S(1)}, bf16[2,2,3,48,384]{4,3,2,1,0:T(8,128)(2,1)S(1)}, u32[]{:S(2)}, u32[]{:S(2)}) collective-permute-start(bf16[2,2,3,48,384]{4,3,2,1,0:T(8,128)(2,1)S(1)} %pad_maximum_fusion.p_one), channel_id=1, source_target_pairs={{0,384},{1,385},{2,386},{3,387},{4,388},{5,389},{6,390},{7,391},{8... | collective-permute-start | bytes 1327112 | tf_op jit(solution)/shard_map/ppermute | solution.py:14
  (16 other events, 229.0 us)

commit v2 on v1

--- a/solution.py
+++ b/solution.py
@@ -30,12 +30,10 @@
 
 def solve(residue, left, right):
     left_vectors, left_inverse, left_values = left
-    right_packed, right_inverse = right
-    tile = residue.shape[0]
+    right_vectors, right_inverse, right_values = right
     first = dot(left_inverse[...], residue.astype(jnp.bfloat16)).astype(jnp.bfloat16)
-    second = dot(first, right_packed[:tile, :])
-    right_values = right_packed[tile:, :].astype(jnp.float32)[:1]
-    third = (second / (left_values[...] + right_values)).astype(jnp.bfloat16)
+    second = dot(first, right_vectors[...])
+    third = (second / (left_values[...] + right_values[...])).astype(jnp.bfloat16)
     fourth = dot(left_vectors[...], third).astype(jnp.bfloat16)
     return dot(fourth, right_inverse[...])
 
@@ -50,24 +48,24 @@
     return chosen.astype(jnp.bfloat16)
 
 
-def first_wave(c, u, p, lam, vm, q, x, xb):
-    value = solve(c[...], (u, p, lam), (vm, q))
+def first_wave(c, u, p, lam, v, q, mu, x, xb):
+    value = solve(c[...], (u, p, lam), (v, q, mu))
     x[...] = value
     xb[...] = value.astype(jnp.bfloat16)
 
 
-def second_wave(info, c, n, below, across, own, b_band, u, p, lam, vm, q, x, xb):
+def second_wave(info, c, n, below, across, own, b_band, u, p, lam, v, q, mu, x, xb):
     slot = info[1]
     left = either(slot == 0, across[...], own[...])
     residue = c[...] - dot(tile_of(n, slot), below[...]) - dot(left, tile_of(b_band, slot))
-    value = solve(residue, (u, p, lam), (vm, q))
+    value = solve(residue, (u, p, lam), (v, q, mu))
     x[...] = value
     xb[...] = value.astype(jnp.bfloat16)
 
 
 def third_wave(
-    info, c, a, n, col_two, row_two, col_one, row_one, own, b_band, b_above, u, p, lam, vm, q,
-    x, down, across,
+    info, c, a, n, col_two, row_two, col_one, row_one, own, b_band, b_above, u, p, lam, v, q, mu,
+    x, *parts,
 ):
     slot = info[2]
     tile = x.shape[0]
@@ -80,12 +78,16 @@
         - dot(a_tile, col_one[...])
         - dot(left, tile_of(b_above, slot))
     )
-    value = solve(residue, (u, p, lam), (vm, q))
+    value = solve(residue, (u, p, lam), (v, q, mu))
     x[...] = value
     packed = value.astype(jnp.bfloat16)
-    down[0] = packed
-    down[1] = col_one[...]
-    down[2] = col_two[...]
+    across = parts[-1]
+    quarter = tile // 4
+    for index in range(4):
+        rows = slice(index * quarter, (index + 1) * quarter)
+        parts[index][0] = packed[rows]
+        parts[index][1] = col_one[rows, :]
+        parts[index][2] = col_two[rows, :]
     across[0] = packed
     across[1] = left
     across[2] = row_two[...]
@@ -186,21 +188,19 @@
     return x, got
 
 
-def col_spread(x, row, col):
-    tile = x.shape[1]
-    plane, z = row // 8, row % 8
-    relative = plane ^ (col // 4)
-    half, quarter = tile // 2, tile // 4
+def col_spread(quarters, row, col):
+    z = row % 8
+    relative = (row // 8) ^ (col // 4)
     diagonal = [(k // 8, k % 8, k // 2) for k in range(ROWS)]
-    got = send(x[:, half:], [((p * 8 + s, c), ((3 - p) * 8 + s, c)) for p, s, c in diagonal])
-    part = jnp.where(relative == 0, x[:, :half], got)
-    pairs = []
-    for p, s, c in diagonal:
-        pairs.append(((p * 8 + s, c), ((p ^ 1) * 8 + s, c)))
-        pairs.append((((3 - p) * 8 + s, c), (((3 - p) ^ 1) * 8 + s, c)))
-    got = send(part[:, quarter:], pairs)
-    first = (relative == 0) | (relative == 3)
-    part = jnp.where(first, part[:, :quarter], got)
+    got = []
+    for index, flip in ((1, 1), (2, 3), (3, 2)):
+        pairs = [((p * 8 + s, c), ((p ^ flip) * 8 + s, c)) for p, s, c in diagonal]
+        got.append(send(quarters[index], pairs))
+    part = jnp.where(
+        relative == 0,
+        quarters[0],
+        jnp.where(relative == 1, got[0], jnp.where(relative == 3, got[1], got[2])),
+    )
     base = 2 * (col % 4)
     pairs = [((q * 8 + s, c), (q * 8 + 7 - s, c)) for _, s, c in diagonal for q in range(4)]
     got = send(part, pairs)
@@ -218,7 +218,7 @@
     both = jnp.stack([part, got])
     near = [((r, c), (r ^ 8, c)) for r, c in every]
     far = [((r, c), (r ^ 24, c)) for r, c in every]
-    piece = tile // 8
+    piece = part.shape[1] // 2
     p_one = both[:, :, :piece]
     q_one = both[:, :, piece:]
     p_one = jnp.stack([p_one, send(p_one, near)])
@@ -248,13 +248,23 @@
     left = (a_vectors, a_inverse, a_values.astype(jnp.float32)[:, None])
     square = jax.ShapeDtypeStruct((tile, tile), jnp.bfloat16)
     exact = jax.ShapeDtypeStruct((tile, tile), jnp.float32)
+    strip = jax.ShapeDtypeStruct((3, tile // 4, tile), jnp.bfloat16)
     three = jax.ShapeDtypeStruct((3, tile, tile), jnp.bfloat16)
 
-    packed = jnp.concatenate([b_vectors, jnp.broadcast_to(b_values[None], (16, tile))])
-    packed_one = send(packed, band((0, 1), 1, 0))
+    vectors_one = send(b_vectors, band((0, 1), 1, 0))
     inverse_one = send(b_inverse, band((0, 1), 1, 0))
-    packed_two = send(packed_one, band((1, 2), 1, 0))
+    values_one = send(b_values, band((0, 1), 1, 0))
+    vectors_two = send(vectors_one, band((1, 2), 1, 0))
     inverse_two = send(inverse_one, band((1, 2), 1, 0))
+    values_two = send(values_one, band((1, 2), 1, 0))
+    rights = [
+        (vectors, inverse, values.astype(jnp.float32)[None])
+        for vectors, inverse, values in (
+            (b_vectors, b_inverse, b_values),
+            (vectors_one, inverse_one, values_one),
+            (vectors_two, inverse_two, values_two),
+        )
+    ]
     b_band = send(b_upper, band((-2, -1, 0), 2, 0))
     a_next = send(a_upper, [((r, c), (r, c - 1)) for r in range(ROWS) for c in range(1, COLS)])
 
@@ -267,24 +277,24 @@
 
     x_two, solved_two = run(
         "K2", first_wave, (exact, square), 4, None,
-        c_two.astype(jnp.bfloat16), *left, packed_two, inverse_two,
+        c_two.astype(jnp.bfloat16), *left, *rights[2],
     )
     below = send(solved_two, band((2, 3), -1, 0))
     row_two = send(solved_two, band((2, 3), 0, 1))
     col_two = send(solved_two, band((2, 3), -2, 0))
     x_one, solved_one = run(
         "K1", second_wave, (exact, square), 6, info,
-        c_one, a_next, below, row_two, solved_two, b_band, *left, packed_one, inverse_one,
+        c_one, a_next, below, row_two, solved_two, b_band, *left, *rights[1],
     )
     col_one = send(solved_one, band((1, 2), -1, 0))
     row_one = send(solved_one, band((2,), 0, 1))
-    x_zero, down, across = run(
-        "K0", third_wave, (exact, three, three), 8, info,
+    x_zero, *quarters, across = run(
+        "K0", third_wave, (exact, *[strip] * 4, three), 8, info,
         c_zero, a_upper, a_next, col_two, row_two, col_one, row_one, solved_one,
-        b_band, b_above, *left, packed, b_inverse,
+        b_band, b_above, *left, *rights[0],
     )
     offset = col - row // 2
-    pieces = col_spread(down, row, col)
+    pieces = col_spread(quarters, row, col)
     across, flipped = row_tree(across, offset)
     return run(
         "KF", last_update, (jax.ShapeDtypeStruct(c_matrix.shape, jnp.float32),), 12, info,

time: 165 us -> 185 us (1.12)
  the two profiles are of different devices: /device:TPU:62 before, /device:TPU:60 now
where the time goes in v2:
time: 185 us; the launch traced here: 184 us
  waiting for transfers between devices  92.7 us (50%)
  starting transfers between devices  57.3 us (31%)
  Pallas kernels  13.2 us (7%)
  local copies, waits for them, and re-layouts  11.4 us (6%)
  other arithmetic  7.99 us (4%)
    ppermute x29, waiting for transfers between devices, send(): return lax.ppermute(x, ('row', 'col'), flat)  92.7 us
    ppermute x29, starting transfers between devices, send(): return lax.ppermute(x, ('row', 'col'), flat)  57.3 us
    pallas_call x4, Pallas kernels, run(): pl.pallas_call(kernel, out_shape=outs, in_specs=[pl.BlockSpec(memory_spac...  13.2 us
    unnamed x60, local copies, waits for them, and re-layouts  9.2 us
    select_n x3, other arithmetic, row_tree(): x = jnp.where(takes, got, x)  5.73 us
  transfers between devices with their start and end apart: 29, of which 6 were waited for; matrix products, arithmetic and copies ran while one was open for 4% of the time, Pallas kernels for 3%

profile of v2, /device:TPU:60, one launch (start us, length us, event | category | flops | bytes accessed | tf_op | source)
XLA Modules:
  0.0 183.6 jit_solution(13853885626298715578)
XLA Ops:
  2.8 2.7 %collective-permute-start = (bf16[384,768]{1,0:T(8,128)(2,1)}, bf16[384,768]{1,0:T(8,128)(2,1)S(1)}, u32[]{:S(2)}, u32[]{:S(2)}) collective-permute-start(bf16[384,768]{1,0:T(8,128)(2,1)} %a.3), channel_id=1, source_target_pairs={{1,0},{2,1},{3,2},{4,3},{5,4},{6,5},{7,6},{8,7},{9,8},{10,9},{11,1... | collective-permute-start | bytes 1769480 | tf_op jit(solution)/shard_map/ppermute | solution.py:14
  11.6 1.9 %shard_map.91 = (f32[384,384]{1,0:T(8,128)S(1)}, bf16[384,384]{1,0:T(8,128)(2,1)}) custom-call(bf16[384,384]{1,0:T(8,128)(2,1)S(1)} %dynamic-slice_convert_fusion.c, bf16[384,384]{1,0:T(8,128)(2,1)S(1)} %copy-done.4, bf16[384,384]{1,0:T(8,128)(2,1)S(1)} %copy-done.6, f32[384,1]{1,0:T(8,128)S(1)} %reshape.4.lam, ...), custom_call_target="tpu_custom_call" | custom-call | flops 452984832 | bytes 2362368 | tf_op jit(solution)/shard_map/pallas_call | solution.py:157
  15.7 4.3 %collective-permute-start.1 = (bf16[384,768]{1,0:T(8,128)(2,1)}, bf16[384,768]{1,0:T(8,128)(2,1)S(1)}, u32[]{:S(2)}, u32[]{:S(2)}) collective-permute-start(bf16[384,768]{1,0:T(8,128)(2,1)} %b.1), channel_id=1, source_target_pairs={{0,16},{1,17},{2,18},{3,19},{4,20},{5,21},{6,22},{7,23},{8,24},{9,... | collective-permute-start | bytes 1769480 | tf_op jit(solution)/shard_map/ppermute | solution.py:14
  24.7 2.7 %shard_map.92 = (f32[384,384]{1,0:T(8,128)S(1)}, bf16[384,384]{1,0:T(8,128)(2,1)S(1)}) custom-call(s32[14]{0:T(128)S(1)} %stack.74.info, f32[384,384]{1,0:T(8,128)S(1)} %get-tuple-element.25.c, bf16[384,768]{1,0:T(8,128)(2,1)S(1)} %collective-permute-done.n, bf16[384,384]{1,0:T(8,128)(2,1)S(1)} %copy-done.22, bf16[384,384]{1,0:T(8,128)(2,1)S(1)} %copy-done.9, ...), custom_call_target="tpu_custom_call" | custom-call | flops 679477248 | bytes 4721664 | tf_op jit(solution)/shard_map/pallas_call | solution.py:157
  29.6 10.4 %collective-permute-done.1.b_above = bf16[384,768]{1,0:T(8,128)(2,1)S(1)} collective-permute-done((bf16[384,768]{1,0:T(8,128)(2,1)}, bf16[384,768]{1,0:T(8,128)(2,1)S(1)}, u32[]{:S(2)}, u32[]{:S(2)}) %collective-permute-start.1) | collective-permute-done | bytes 589856 | tf_op jit(solution)/shard_map/ppermute | solution.py:14
  40.1 3.6 %shard_map.93 = (f32[384,384]{1,0:T(8,128)S(1)}, bf16[3,96,384]{2,1,0:T(8,128)(2,1)S(1)}, bf16[3,96,384]{2,1,0:T(8,128)(2,1)}, bf16[3,96,384]{2,1,0:T(8,128)(2,1...) custom-call(s32[14]{0:T(128)S(1)} %stack.74.info, f32[384,384]{1,0:T(8,128)S(1)} %get-tuple-element.26.c, ...), custom_call_target="tpu_custom_call" | custom-call | flops 905969664 | bytes 7965696 | tf_op jit(solution)/shard_map/pallas_call | solution.py:157
  45.9 1.6 collective-permute-start.25
  47.5 2.2 %broadcast_select_fusion = bf16[3,384,384]{2,1,0:T(8,128)(2,1)} fusion(bf16[3,384,384]{2,1,0:T(8,128)(2,1)} %collective-permute-done.25, bf16[3,384,384]{2,1,0:T(8,128)(2,1)} %get-tuple-element.21, pred[]{:T(512)S(6)} %and.127), kind=kLoop, calls=%fused_computation | loop fusion | flops 442368 | bytes 2654209 | tf_op jit(solution)/shard_map/jit(_where)/select_n | solution.py:181
  49.8 1.6 collective-permute-start.26
  54.1 1.4 collective-permute-start.17
  57.2 2.2 %broadcast_select_fusion.1 = bf16[3,384,384]{2,1,0:T(8,128)(2,1)} fusion(bf16[3,384,384]{2,1,0:T(8,128)(2,1)} %collective-permute-done.26, bf16[3,384,384]{2,1,0:T(8,128)(2,1)} %broadcast_select_fusion, pred[]{:T(512)S(6)} %and.125), kind=kLoop, calls=%fused_computation.1 | loop fusion | flops 442368 | bytes 2654209 | tf_op jit(solution)/shard_map/jit(_where)/select_n | solution.py:181
  62.1 55.0 %collective-permute-done.19 = bf16[3,96,384]{2,1,0:T(8,128)(2,1)} collective-permute-done((bf16[3,96,384]{2,1,0:T(8,128)(2,1)S(1)}, bf16[3,96,384]{2,1,0:T(8,128)(2,1)}, u32[]{:S(2)}, u32[]{:S(2)}) %collective-permute-start.19) | collective-permute-done | bytes 221216 | tf_op jit(solution)/shard_map/ppermute | solution.py:14
  118.1 1.9 %collective-permute-start.20 = (bf16[3,96,384]{2,1,0:T(8,128)(2,1)S(1)}, bf16[3,96,384]{2,1,0:T(8,128)(2,1)S(1)}, u32[]{:S(2)}, u32[]{:S(2)}) collective-permute-start(bf16[3,96,384]{2,1,0:T(8,128)(2,1)S(1)} %broadcast_select_fusion.4), channel_id=1, source_target_pairs={{0,16},{1,17},{2,18},{3,19},{4,20},{5,21},{6,22},{7,23},{8,24},{9,... | collective-permute-start | bytes 663560 | tf_op jit(solution)/shard_map/ppermute | solution.py:14
  120.1 5.9 %collective-permute-done.20 = bf16[3,96,384]{2,1,0:T(8,128)(2,1)S(1)} collective-permute-done((bf16[3,96,384]{2,1,0:T(8,128)(2,1)S(1)}, bf16[3,96,384]{2,1,0:T(8,128)(2,1)S(1)}, u32[]{:S(2)}, u32[]{:S(2)}) %collective-permute-start.20) | collective-permute-done | bytes 221216 | tf_op jit(solution)/shard_map/ppermute | solution.py:14
  126.0 18.5 %collective-permute-start.21 = (bf16[2,3,48,384]{3,2,1,0:T(8,128)(2,1)S(1)}, bf16[2,3,48,384]{3,2,1,0:T(8,128)(2,1)S(1)}, u32[]{:S(2)}, u32[]{:S(2)}) collective-permute-start(bf16[2,3,48,384]{3,2,1,0:T(8,128)(2,1)S(1)} %get-tuple-element.28), channel_id=1, source_target_pairs={{0,128},{1,129},{2,130},{3,131},{4,132},{5,133},{6,134},{7,135},{8... | collective-permute-start | bytes 663560 | tf_op jit(solution)/shard_map/ppermute | solution.py:14
  145.9 1.5 collective-permute-start.28
  147.4 3.8 %collective-permute-start.23 = (bf16[2,3,48,384]{3,2,1,0:T(8,128)(2,1)S(1)}, bf16[2,3,48,384]{3,2,1,0:T(8,128)(2,1)S(1)}, u32[]{:S(2)}, u32[]{:S(2)}) collective-permute-start(bf16[2,3,48,384]{3,2,1,0:T(8,128)(2,1)S(1)} %get-tuple-element.27), channel_id=1, source_target_pairs={{0,384},{1,385},{2,386},{3,387},{4,388},{5,389},{6,390},{7,391},{8... | collective-permute-start | bytes 663560 | tf_op jit(solution)/shard_map/ppermute | solution.py:14
  151.1 1.9 %collective-permute-start.2 = (bf16[384,768]{1,0:T(8,128)(2,1)S(1)}, bf16[384,768]{1,0:T(8,128)(2,1)S(1)}, u32[]{:S(2)}, u32[]{:S(2)}) collective-permute-start(bf16[384,768]{1,0:T(8,128)(2,1)S(1)} %collective-permute-done.1.b_above), channel_id=1, source_target_pairs={{1,17},{2,18},{3,19},{4,20},{5,21},{6,22},{7,23},{8,24},{9,25},{10... | collective-permute-start | bytes 1769480 | tf_op jit(solution)/shard_map/ppermute | solution.py:14
  153.1 2.1 %collective-permute-start.22 = (bf16[2,2,3,48,384]{4,3,2,1,0:T(8,128)(2,1)S(1)}, bf16[2,2,3,48,384]{4,3,2,1,0:T(8,128)(2,1)S(1)}, u32[]{:S(2)}, u32[]{:S(2)}) collective-permute-start(bf16[2,2,3,48,384]{4,3,2,1,0:T(8,128)(2,1)S(1)} %pad_maximum_fusion.p_one), channel_id=1, source_target_pairs={{0,384},{1,385},{2,386},{3,387},{4,388},{5,389},{6,390},{7,391},{8... | collective-permute-start | bytes 1327112 | tf_op jit(solution)/shard_map/ppermute | solution.py:14
  155.2 13.1 %collective-permute-done.23 = bf16[2,3,48,384]{3,2,1,0:T(8,128)(2,1)S(1)} collective-permute-done((bf16[2,3,48,384]{3,2,1,0:T(8,128)(2,1)S(1)}, bf16[2,3,48,384]{3,2,1,0:T(8,128)(2,1)S(1)}, u32[]{:S(2)}, u32[]{:S(2)}) %collective-permute-start.23) | collective-permute-done | bytes 221216 | tf_op jit(solution)/shard_map/ppermute | solution.py:14
  168.4 1.9 %collective-permute-start.24 = (bf16[2,2,3,48,384]{4,3,2,1,0:T(8,128)(2,1)S(1)}, bf16[2,2,3,48,384]{4,3,2,1,0:T(8,128)(2,1)S(1)}, u32[]{:S(2)}, u32[]{:S(2)}) collective-permute-start(bf16[2,2,3,48,384]{4,3,2,1,0:T(8,128)(2,1)S(1)} %pad_maximum_fusion.1.q_one), channel_id=1, source_target_pairs={{0,128},{1,129},{2,130},{3,131},{4,132},{5,133},{6,134},{7,135},{8... | collective-permute-start | bytes 1327112 | tf_op jit(solution)/shard_map/ppermute | solution.py:14
  170.3 2.7 %collective-permute-done.22.p_two = bf16[2,2,3,48,384]{4,3,2,1,0:T(8,128)(2,1)S(1)} collective-permute-done((bf16[2,2,3,48,384]{4,3,2,1,0:T(8,128)(2,1)S(1)}, bf16[2,2,3,48,384]{4,3,2,1,0:T(8,128)(2,1)S(1)}, u32[]{:S(2)}, u32[]{:S(2)}) %collective-permute-start.22) | collective-permute-done | bytes 442400 | tf_op jit(solution)/shard_map/ppermute | solution.py:14
  173.0 5.5 %collective-permute-done.24.q_two = bf16[2,2,3,48,384]{4,3,2,1,0:T(8,128)(2,1)S(1)} collective-permute-done((bf16[2,2,3,48,384]{4,3,2,1,0:T(8,128)(2,1)S(1)}, bf16[2,2,3,48,384]{4,3,2,1,0:T(8,128)(2,1)S(1)}, u32[]{:S(2)}, u32[]{:S(2)}) %collective-permute-start.24) | collective-permute-done | bytes 442400 | tf_op jit(solution)/shard_map/ppermute | solution.py:14
  178.6 5.0 %shard_map.94 = f32[384,768]{1,0:T(8,128)} custom-call(s32[14]{0:T(128)S(1)} %stack.74.info, f32[384,768]{1,0:T(8,128)S(1)} %copy-done, bf16[384,768]{1,0:T(8,128)(2,1)S(1)} %copy-done.1, bf16[384,768]{1,0:T(8,128)(2,1)S(1)} %collective-permute-done.n, bf16[384,768]{1,0:T(8,128)(2,1)} %b.1, bf16[384,768]{1,0:T(8,128)(2,1)S(1)} %collective-permute-done.1.b_above, ...), custom_call_target="tpu_custom_call" | custom-call | flops 1358954496 | bytes 10616832 | tf_op jit(solution)/shard_map/pallas_call | solution.py:157
  (114 shorter events, 29.2 us)
Async XLA Ops:
  1.4 8.2 %collective-permute-start.4 = (bf16[384,384]{1,0:T(8,128)(2,1)S(1)}, bf16[384,384]{1,0:T(8,128)(2,1)S(1)}, u32[]{:S(2)}, u32[]{:S(2)}) collective-permute-start(bf16[384,384]{1,0:T(8,128)(2,1)S(1)} %collective-permute-done.3.v), channel_id=1, source_target_pairs={{16,32},{32,48},{49,65},{65,81},{82,98},{98,114},{115,131},{131,14... | collective-permute-start | bytes 884744 | tf_op jit(solution)/shard_map/ppermute | solution.py:14
  2.1 7.5 %collective-permute-start.6 = (bf16[384,384]{1,0:T(8,128)(2,1)S(1)}, bf16[384,384]{1,0:T(8,128)(2,1)S(1)}, u32[]{:S(2)}, u32[]{:S(2)}) collective-permute-start(bf16[384,384]{1,0:T(8,128)(2,1)S(1)} %collective-permute-done.5.q), channel_id=1, source_target_pairs={{16,32},{32,48},{49,65},{65,81},{82,98},{98,114},{115,131},{131,14... | collective-permute-start | bytes 884744 | tf_op jit(solution)/shard_map/ppermute | solution.py:14
  2.8 17.7 %collective-permute-start = (bf16[384,768]{1,0:T(8,128)(2,1)}, bf16[384,768]{1,0:T(8,128)(2,1)S(1)}, u32[]{:S(2)}, u32[]{:S(2)}) collective-permute-start(bf16[384,768]{1,0:T(8,128)(2,1)} %a.3), channel_id=1, source_target_pairs={{1,0},{2,1},{3,2},{4,3},{5,4},{6,5},{7,6},{8,7},{9,8},{10,9},{11,1... | collective-permute-start | bytes 1769480 | tf_op jit(solution)/shard_map/ppermute | solution.py:14
  5.5 15.8 %collective-permute-start.12 = (bf16[384,768]{1,0:T(8,128)(2,1)}, bf16[384,768]{1,0:T(8,128)(2,1)S(1)}, u32[]{:S(2)}, u32[]{:S(2)}) collective-permute-start(bf16[384,768]{1,0:T(8,128)(2,1)} %b.1), channel_id=1, source_target_pairs={{0,32},{1,33},{17,49},{33,65},{34,66},{50,82},{66,98},{67,99},{83,... | collective-permute-start | bytes 1769480 | tf_op jit(solution)/shard_map/ppermute | solution.py:14
  6.9 2.7 %collective-permute-start.8 = (bf16[384]{0:T(512)(128)(2,1)S(1)}, bf16[384]{0:T(512)(128)(2,1)S(1)}, u32[]{:S(2)}, u32[]{:S(2)}) collective-permute-start(bf16[384]{0:T(512)(128)(2,1)S(1)} %collective-permute-done.7), channel_id=1, source_target_pairs={{16,32},{32,48},{49,65},{65,81},{82,98},{98,114},{115,131},{131,14... | collective-permute-start | bytes 2312 | tf_op jit(solution)/shard_map/ppermute | solution.py:14
  14.3 7.0 %collective-permute-start.11 = (bf16[384,384]{1,0:T(8,128)(2,1)}, bf16[384,384]{1,0:T(8,128)(2,1)S(1)}, u32[]{:S(2)}, u32[]{:S(2)}) collective-permute-start(bf16[384,384]{1,0:T(8,128)(2,1)} %get-tuple-element.15.own), channel_id=1, source_target_pairs={{32,16},{48,32},{65,49},{81,65},{98,82},{114,98},{131,115},{147,13... | collective-permute-start | bytes 884744 | tf_op jit(solution)/shard_map/ppermute | solution.py:14
  15.0 7.0 %collective-permute-start.10 = (bf16[384,384]{1,0:T(8,128)(2,1)}, bf16[384,384]{1,0:T(8,128)(2,1)S(1)}, u32[]{:S(2)}, u32[]{:S(2)}) collective-permute-start(bf16[384,384]{1,0:T(8,128)(2,1)} %get-tuple-element.15.own), channel_id=1, source_target_pairs={{32,33},{48,49},{65,66},{81,82},{98,99},{114,115},{131,132},{147,1... | collective-permute-start | bytes 884744 | tf_op jit(solution)/shard_map/ppermute | solution.py:14
  15.7 24.4 %collective-permute-start.1 = (bf16[384,768]{1,0:T(8,128)(2,1)}, bf16[384,768]{1,0:T(8,128)(2,1)S(1)}, u32[]{:S(2)}, u32[]{:S(2)}) collective-permute-start(bf16[384,768]{1,0:T(8,128)(2,1)} %b.1), channel_id=1, source_target_pairs={{0,16},{1,17},{2,18},{3,19},{4,20},{5,21},{6,22},{7,23},{8,24},{9,... | collective-permute-start | bytes 1769480 | tf_op jit(solution)/shard_map/ppermute | solution.py:14
  20.5 19.6 %collective-permute-start.9 = (bf16[384,384]{1,0:T(8,128)(2,1)}, bf16[384,384]{1,0:T(8,128)(2,1)S(1)}, u32[]{:S(2)}, u32[]{:S(2)}) collective-permute-start(bf16[384,384]{1,0:T(8,128)(2,1)} %get-tuple-element.15.own), channel_id=1, source_target_pairs={{32,0},{48,16},{65,33},{81,49},{98,66},{114,82},{131,99},{147,115}... | collective-permute-start | bytes 884744 | tf_op jit(solution)/shard_map/ppermute | solution.py:14
  28.2 11.8 %collective-permute-start.14 = (bf16[384,384]{1,0:T(8,128)(2,1)S(1)}, bf16[384,384]{1,0:T(8,128)(2,1)S(1)}, u32[]{:S(2)}, u32[]{:S(2)}) collective-permute-start(bf16[384,384]{1,0:T(8,128)(2,1)S(1)} %get-tuple-element.16.own), channel_id=1, source_target_pairs={{32,33},{65,66},{98,99},{131,132},{164,165},{197,198},{230,231},{2... | collective-permute-start | bytes 884744 | tf_op jit(solution)/shard_map/ppermute | solution.py:14
  28.9 11.1 %collective-permute-start.13 = (bf16[384,384]{1,0:T(8,128)(2,1)S(1)}, bf16[384,384]{1,0:T(8,128)(2,1)S(1)}, u32[]{:S(2)}, u32[]{:S(2)}) collective-permute-start(bf16[384,384]{1,0:T(8,128)(2,1)S(1)} %get-tuple-element.16.own), channel_id=1, source_target_pairs={{16,0},{32,16},{49,33},{65,49},{82,66},{98,82},{115,99},{131,115},... | collective-permute-start | bytes 884744 | tf_op jit(solution)/shard_map/ppermute | solution.py:14
  49.8 7.5 %collective-permute-start.26 = (bf16[3,384,384]{2,1,0:T(8,128)(2,1)}, bf16[3,384,384]{2,1,0:T(8,128)(2,1)}, u32[]{:S(2)}, u32[]{:S(2)}) collective-permute-start(bf16[3,384,384]{2,1,0:T(8,128)(2,1)} %broadcast_select_fusion), channel_id=1, source_target_pairs={{0,4},{8,12},{16,20},{24,28},{33,37},{41,45},{49,53},{57,61},{66,7... | collective-permute-start | bytes 2654216 | tf_op jit(solution)/shard_map/ppermute | solution.py:14
  51.4 4.1 %collective-permute-start.15 = (bf16[3,96,384]{2,1,0:T(8,128)(2,1)}, bf16[3,96,384]{2,1,0:T(8,128)(2,1)}, u32[]{:S(2)}, u32[]{:S(2)}) collective-permute-start(bf16[3,96,384]{2,1,0:T(8,128)(2,1)} %get-tuple-element.18), channel_id=1, source_target_pairs={{0,128},{16,144},{33,161},{49,177},{66,194},{82,210},{99,227},{115... | collective-permute-start | bytes 663560 | tf_op jit(solution)/shard_map/ppermute | solution.py:14
  52.7 2.7 %collective-permute-start.16 = (bf16[3,96,384]{2,1,0:T(8,128)(2,1)}, bf16[3,96,384]{2,1,0:T(8,128)(2,1)}, u32[]{:S(2)}, u32[]{:S(2)}) collective-permute-start(bf16[3,96,384]{2,1,0:T(8,128)(2,1)} %get-tuple-element.19), channel_id=1, source_target_pairs={{0,384},{16,400},{33,417},{49,433},{66,450},{82,466},{99,483},{115... | collective-permute-start | bytes 663560 | tf_op jit(solution)/shard_map/ppermute | solution.py:14
  56.6 4.2 %collective-permute-start.18 = (bf16[3,96,384]{2,1,0:T(8,128)(2,1)S(1)}, bf16[3,96,384]{2,1,0:T(8,128)(2,1)S(1)}, u32[]{:S(2)}, u32[]{:S(2)}) collective-permute-start(bf16[3,96,384]{2,1,0:T(8,128)(2,1)S(1)} %select_select_fusion), channel_id=1, source_target_pairs={{0,112},{128,240},{256,368},{384,496},{16,96},{144,224},{272,352},... | collective-permute-start | bytes 663560 | tf_op jit(solution)/shard_map/ppermute | solution.py:14
  59.4 85.1 %collective-permute-start.27 = (bf16[3,384,384]{2,1,0:T(8,128)(2,1)}, bf16[3,384,384]{2,1,0:T(8,128)(2,1)}, u32[]{:S(2)}, u32[]{:S(2)}) collective-permute-start(bf16[3,384,384]{2,1,0:T(8,128)(2,1)} %broadcast_select_fusion.1), channel_id=1, source_target_pairs={{0,2},{4,6},{8,10},{12,14},{16,18},{20,22},{24,26},{28,30},{33,35}... | collective-permute-start | bytes 2654216 | tf_op jit(solution)/shard_map/ppermute | solution.py:14
  60.8 56.4 %collective-permute-start.19 = (bf16[3,96,384]{2,1,0:T(8,128)(2,1)S(1)}, bf16[3,96,384]{2,1,0:T(8,128)(2,1)}, u32[]{:S(2)}, u32[]{:S(2)}) collective-permute-start(bf16[3,96,384]{2,1,0:T(8,128)(2,1)S(1)} %broadcast_select_fusion.3), channel_id=1, source_target_pairs={{0,32},{112,80},{128,160},{240,208},{256,288},{368,336},{384,416},... | collective-permute-start | bytes 663560 | tf_op jit(solution)/shard_map/ppermute | solution.py:14
  118.1 7.8 %collective-permute-start.20 = (bf16[3,96,384]{2,1,0:T(8,128)(2,1)S(1)}, bf16[3,96,384]{2,1,0:T(8,128)(2,1)S(1)}, u32[]{:S(2)}, u32[]{:S(2)}) collective-permute-start(bf16[3,96,384]{2,1,0:T(8,128)(2,1)S(1)} %broadcast_select_fusion.4), channel_id=1, source_target_pairs={{0,16},{1,17},{2,18},{3,19},{4,20},{5,21},{6,22},{7,23},{8,24},{9,... | collective-permute-start | bytes 663560 | tf_op jit(solution)/shard_map/ppermute | solution.py:14
  126.0 27.1 %collective-permute-start.21 = (bf16[2,3,48,384]{3,2,1,0:T(8,128)(2,1)S(1)}, bf16[2,3,48,384]{3,2,1,0:T(8,128)(2,1)S(1)}, u32[]{:S(2)}, u32[]{:S(2)}) collective-permute-start(bf16[2,3,48,384]{3,2,1,0:T(8,128)(2,1)S(1)} %get-tuple-element.28), channel_id=1, source_target_pairs={{0,128},{1,129},{2,130},{3,131},{4,132},{5,133},{6,134},{7,135},{8... | collective-permute-start | bytes 663560 | tf_op jit(solution)/shard_map/ppermute | solution.py:14
  145.9 32.7 %collective-permute-start.28 = (bf16[3,384,384]{2,1,0:T(8,128)(2,1)S(1)}, bf16[3,384,384]{2,1,0:T(8,128)(2,1)S(1)}, u32[]{:S(2)}, u32[]{:S(2)}) collective-permute-start(bf16[3,384,384]{2,1,0:T(8,128)(2,1)S(1)} %broadcast_select_fusion.2.across), channel_id=1, source_target_pairs={{0,1},{2,3},{4,5},{6,7},{8,9},{10,11},{12,13},{14,15},{16,17},{18,... | collective-permute-start | bytes 2654216 | tf_op jit(solution)/shard_map/ppermute | solution.py:14
  147.4 20.9 %collective-permute-start.23 = (bf16[2,3,48,384]{3,2,1,0:T(8,128)(2,1)S(1)}, bf16[2,3,48,384]{3,2,1,0:T(8,128)(2,1)S(1)}, u32[]{:S(2)}, u32[]{:S(2)}) collective-permute-start(bf16[2,3,48,384]{3,2,1,0:T(8,128)(2,1)S(1)} %get-tuple-element.27), channel_id=1, source_target_pairs={{0,384},{1,385},{2,386},{3,387},{4,388},{5,389},{6,390},{7,391},{8... | collective-permute-start | bytes 663560 | tf_op jit(solution)/shard_map/ppermute | solution.py:14
  151.1 19.2 %collective-permute-start.2 = (bf16[384,768]{1,0:T(8,128)(2,1)S(1)}, bf16[384,768]{1,0:T(8,128)(2,1)S(1)}, u32[]{:S(2)}, u32[]{:S(2)}) collective-permute-start(bf16[384,768]{1,0:T(8,128)(2,1)S(1)} %collective-permute-done.1.b_above), channel_id=1, source_target_pairs={{1,17},{2,18},{3,19},{4,20},{5,21},{6,22},{7,23},{8,24},{9,25},{10... | collective-permute-start | bytes 1769480 | tf_op jit(solution)/shard_map/ppermute | solution.py:14
  153.1 19.9 %collective-permute-start.22 = (bf16[2,2,3,48,384]{4,3,2,1,0:T(8,128)(2,1)S(1)}, bf16[2,2,3,48,384]{4,3,2,1,0:T(8,128)(2,1)S(1)}, u32[]{:S(2)}, u32[]{:S(2)}) collective-permute-start(bf16[2,2,3,48,384]{4,3,2,1,0:T(8,128)(2,1)S(1)} %pad_maximum_fusion.p_one), channel_id=1, source_target_pairs={{0,384},{1,385},{2,386},{3,387},{4,388},{5,389},{6,390},{7,391},{8... | collective-permute-start | bytes 1327112 | tf_op jit(solution)/shard_map/ppermute | solution.py:14
  168.4 10.2 %collective-permute-start.24 = (bf16[2,2,3,48,384]{4,3,2,1,0:T(8,128)(2,1)S(1)}, bf16[2,2,3,48,384]{4,3,2,1,0:T(8,128)(2,1)S(1)}, u32[]{:S(2)}, u32[]{:S(2)}) collective-permute-start(bf16[2,2,3,48,384]{4,3,2,1,0:T(8,128)(2,1)S(1)} %pad_maximum_fusion.1.q_one), channel_id=1, source_target_pairs={{0,128},{1,129},{2,130},{3,131},{4,132},{5,133},{6,134},{7,135},{8... | collective-permute-start | bytes 1327112 | tf_op jit(solution)/shard_map/ppermute | solution.py:14
  (35 other events, 247.3 us)

commit v3 on v2

--- a/solution.py
+++ b/solution.py
@@ -54,17 +54,17 @@
     xb[...] = value.astype(jnp.bfloat16)
 
 
-def second_wave(info, c, n, below, across, own, b_band, u, p, lam, v, q, mu, x, xb):
+def second_wave(info, c, n, below, across, own, b_wave, u, p, lam, v, q, mu, x, xb):
     slot = info[1]
     left = either(slot == 0, across[...], own[...])
-    residue = c[...] - dot(tile_of(n, slot), below[...]) - dot(left, tile_of(b_band, slot))
+    residue = c[...] - dot(tile_of(n, slot), below[...]) - dot(left, b_wave[...])
     value = solve(residue, (u, p, lam), (v, q, mu))
     x[...] = value
     xb[...] = value.astype(jnp.bfloat16)
 
 
 def third_wave(
-    info, c, a, n, col_two, row_two, col_one, row_one, own, b_band, b_above, u, p, lam, v, q, mu,
+    info, c, a, n, col_two, row_two, col_one, row_one, own, b_two, b_above, u, p, lam, v, q, mu,
     x, *parts,
 ):
     slot = info[2]
@@ -74,7 +74,7 @@
     residue = (
         c[...]
         - dot(tile_of(n, slot), col_two[...])
-        - dot(row_two[...], tile_of(b_band, slot))
+        - dot(row_two[...], b_two[...])
         - dot(a_tile, col_one[...])
         - dot(left, tile_of(b_above, slot))
     )
@@ -90,11 +90,11 @@
         parts[index][2] = col_two[rows, :]
     across[0] = packed
     across[1] = left
-    across[2] = row_two[...]
 
 
 def last_update(
     info, c, a, n, b, b_above, b_above_two, p_one, p_two, q_one, q_two, across, flipped,
+    early, early_flipped,
     x_two, x_one, x_zero, out, down,
 ):
     tile = c.shape[0]
@@ -118,13 +118,14 @@
                         )
                         down[member, wave, at, :] = second[slot, index, wave]
 
-    def update(member, source):
+    def update(member, source, source_two):
         span = slice(member * tile, (member + 1) * tile)
         change = dot(a_tiles[member][...], down[member, 0])
         for wave in (1, 2):
             change += dot(a_tiles[member + wave][...], down[member, wave])
-        for wave in range(3):
+        for wave in range(2):
             change += dot(source[wave], b_tiles[wave][:, span])
+        change += dot(source_two[0], b_tiles[2][:, span])
         out[:, span] = c[:, span] - change
 
     for member in range(2):
@@ -132,11 +133,11 @@
 
         @pl.when((where < member) & (info[13] == 0))
         def _():
-            update(member, across)
+            update(member, across, early)
 
         @pl.when((where < member) & (info[13] == 1))
         def _():
-            update(member, flipped)
+            update(member, flipped, early_flipped)
 
         for wave, solved in enumerate((x_zero, x_one, x_two)):
 
@@ -249,7 +250,7 @@
     square = jax.ShapeDtypeStruct((tile, tile), jnp.bfloat16)
     exact = jax.ShapeDtypeStruct((tile, tile), jnp.float32)
     strip = jax.ShapeDtypeStruct((3, tile // 4, tile), jnp.bfloat16)
-    three = jax.ShapeDtypeStruct((3, tile, tile), jnp.bfloat16)
+    pair = jax.ShapeDtypeStruct((2, tile, tile), jnp.bfloat16)
 
     vectors_one = send(b_vectors, band((0, 1), 1, 0))
     inverse_one = send(b_inverse, band((0, 1), 1, 0))
@@ -265,7 +266,9 @@
             (vectors_two, inverse_two, values_two),
         )
     ]
-    b_band = send(b_upper, band((-2, -1, 0), 2, 0))
+    b_tiles = b_upper[:, :tile], b_upper[:, tile:]
+    b_wave = send(jnp.where(d == -1, *b_tiles), band((-1, 0), 2, 0))
+    b_two = send(jnp.where(d == -2, *b_tiles), band((-2, -1), 2, 0))
     a_next = send(a_upper, [((r, c), (r, c - 1)) for r in range(ROWS) for c in range(1, COLS)])
 
     def rows_down(last):
@@ -282,24 +285,25 @@
     below = send(solved_two, band((2, 3), -1, 0))
     row_two = send(solved_two, band((2, 3), 0, 1))
     col_two = send(solved_two, band((2, 3), -2, 0))
+    offset = col - row // 2
+    early, early_flipped = row_tree(row_two[None], offset)
     x_one, solved_one = run(
         "K1", second_wave, (exact, square), 6, info,
-        c_one, a_next, below, row_two, solved_two, b_band, *left, *rights[1],
+        c_one, a_next, below, row_two, solved_two, b_wave, *left, *rights[1],
     )
     col_one = send(solved_one, band((1, 2), -1, 0))
     row_one = send(solved_one, band((2,), 0, 1))
     x_zero, *quarters, across = run(
-        "K0", third_wave, (exact, *[strip] * 4, three), 8, info,
+        "K0", third_wave, (exact, *[strip] * 4, pair), 8, info,
         c_zero, a_upper, a_next, col_two, row_two, col_one, row_one, solved_one,
-        b_band, b_above, *left, *rights[0],
-    )
-    offset = col - row // 2
+        b_two, b_above, *left, *rights[0],
+    )
     pieces = col_spread(quarters, row, col)
     across, flipped = row_tree(across, offset)
     return run(
         "KF", last_update, (jax.ShapeDtypeStruct(c_matrix.shape, jnp.float32),), 12, info,
         c_matrix, a_upper, a_next, b_upper, b_above, b_above_two,
-        *pieces, across, flipped, x_two, x_one, x_zero,
+        *pieces, across, flipped, early, early_flipped, x_two, x_one, x_zero,
         scratch=[pltpu.VMEM((2, 3, tile, tile), jnp.bfloat16)],
     )[0]
 

time: 185 us -> 144 us (0.78)
  the two profiles are of different devices: /device:TPU:60 before, /device:TPU:26 now
where the time goes in v3:
time: 144 us; the launch traced here: 142 us
  waiting for transfers between devices  61.2 us (42%)
  starting transfers between devices  50.6 us (35%)
  Pallas kernels  14.3 us (10%)
  other arithmetic  9.38 us (7%)
  local copies, waits for them, and re-layouts  6.02 us (4%)
    ppermute x34, waiting for transfers between devices, send(): return lax.ppermute(x, ('row', 'col'), flat)  61.2 us
    ppermute x34, starting transfers between devices, send(): return lax.ppermute(x, ('row', 'col'), flat)  50.6 us
    pallas_call x4, Pallas kernels, run(): pl.pallas_call(kernel, out_shape=outs, in_specs=[pl.BlockSpec(memory_spac...  14.3 us
    unnamed x50, local copies, waits for them, and re-layouts  5.68 us
    select_n x6, other arithmetic, row_tree(): x = jnp.where(takes, got, x)  5.04 us
  transfers between devices with their start and end apart: 34, of which 6 were waited for; matrix products, arithmetic and copies ran while one was open for 7% of the time, Pallas kernels for 4%

profile of v3, /device:TPU:26, one launch (start us, length us, event | category | flops | bytes accessed | tf_op | source)
XLA Modules:
  0.0 142.4 jit_solution(2248414317638781917)
XLA Ops:
  2.2 1.9 %collective-permute-start = (bf16[384,768]{1,0:T(8,128)(2,1)}, bf16[384,768]{1,0:T(8,128)(2,1)S(1)}, u32[]{:S(2)}, u32[]{:S(2)}) collective-permute-start(bf16[384,768]{1,0:T(8,128)(2,1)} %a.3), channel_id=1, source_target_pairs={{1,0},{2,1},{3,2},{4,3},{5,4},{6,5},{7,6},{8,7},{9,8},{10,9},{11,1... | collective-permute-start | bytes 1769480 | tf_op jit(solution)/shard_map/ppermute | solution.py:14
  4.2 1.4 collective-permute-start.4
  5.6 1.4 collective-permute-start.6
  6.9 2.0 %broadcast_select_fusion.6 = (bf16[384,384]{1,0:T(8,128)(2,1)}, bf16[384,384]{1,0:T(8,128)(2,1)}) fusion(pred[]{:T(512)S(6)} %eq.65, bf16[384,768]{1,0:T(8,128)(2,1)} %b.1, pred[]{:T(512)S(6)} %eq.64), kind=kLoop, calls=%fused_computation.11 | loop fusion | flops 294912 | bytes 1179650 | tf_op jit(solution)/shard_map/jit(_where)/select_n | solution.py:271
  8.9 1.4 collective-permute-start.12
  11.2 2.9 %shard_map.91 = (f32[384,384]{1,0:T(8,128)S(1)}, bf16[384,384]{1,0:T(8,128)(2,1)}) custom-call(bf16[384,384]{1,0:T(8,128)(2,1)S(1)} %dynamic-slice_convert_fusion.c, bf16[384,384]{1,0:T(8,128)(2,1)S(1)} %copy-done.2, bf16[384,384]{1,0:T(8,128)(2,1)S(1)} %copy-done.4, f32[384,1]{1,0:T(8,128)S(1)} %reshape.4.lam, bf16[384,384]{1,0:T(8,128)(2,1)} %collective-permute-done.4.v, ...), custom_call_target="tpu_custom_call" | custom-call | flops 452984832 | bytes 2362368 | tf_op jit(solution)/shard_map/pallas_call | solution.py:158
  16.3 4.3 %collective-permute-start.1 = (bf16[384,768]{1,0:T(8,128)(2,1)}, bf16[384,768]{1,0:T(8,128)(2,1)S(1)}, u32[]{:S(2)}, u32[]{:S(2)}) collective-permute-start(bf16[384,768]{1,0:T(8,128)(2,1)} %b.1), channel_id=1, source_target_pairs={{0,16},{1,17},{2,18},{3,19},{4,20},{5,21},{6,22},{7,23},{8,24},{9,... | collective-permute-start | bytes 1769480 | tf_op jit(solution)/shard_map/ppermute | solution.py:14
  25.0 2.8 %shard_map.92 = (f32[384,384]{1,0:T(8,128)S(1)}, bf16[384,384]{1,0:T(8,128)(2,1)S(1)}) custom-call(s32[14]{0:T(128)S(1)} %stack.74.info, f32[384,384]{1,0:T(8,128)S(1)} %get-tuple-element.25.c, bf16[384,768]{1,0:T(8,128)(2,1)S(1)} %collective-permute-done.n, bf16[384,384]{1,0:T(8,128)(2,1)S(1)} %copy-done.19, ...), custom_call_target="tpu_custom_call" | custom-call | flops 679477248 | bytes 4426752 | tf_op jit(solution)/shard_map/pallas_call | solution.py:158
  30.0 11.4 %collective-permute-done.1.b_above = bf16[384,768]{1,0:T(8,128)(2,1)S(1)} collective-permute-done((bf16[384,768]{1,0:T(8,128)(2,1)}, bf16[384,768]{1,0:T(8,128)(2,1)S(1)}, u32[]{:S(2)}, u32[]{:S(2)}) %collective-permute-start.1) | collective-permute-done | bytes 589856 | tf_op jit(solution)/shard_map/ppermute | solution.py:14
  41.5 3.6 %shard_map.93 = (f32[384,384]{1,0:T(8,128)S(1)}, bf16[3,96,384]{2,1,0:T(8,128)(2,1)S(1)}, bf16[3,96,384]{2,1,0:T(8,128)(2,1)}, bf16[3,96,384]{2,1,0:T(8,128)(2,1...) custom-call(s32[14]{0:T(128)S(1)} %stack.74.info, f32[384,384]{1,0:T(8,128)S(1)} %get-tuple-element.26.c, ...), custom_call_target="tpu_custom_call" | custom-call | flops 905969664 | bytes 7375872 | tf_op jit(solution)/shard_map/pallas_call | solution.py:158
  46.6 1.5 %collective-permute-start.26 = (bf16[2,384,384]{2,1,0:T(8,128)(2,1)}, bf16[2,384,384]{2,1,0:T(8,128)(2,1)}, u32[]{:S(2)}, u32[]{:S(2)}) collective-permute-start(bf16[2,384,384]{2,1,0:T(8,128)(2,1)} %get-tuple-element.21), channel_id=1, source_target_pairs={{0,8},{16,24},{33,41},{49,57},{66,74},{82,90},{99,107},{115,123},{... | collective-permute-start | bytes 1769480 | tf_op jit(solution)/shard_map/ppermute | solution.py:14
  49.4 1.4 collective-permute-start.17
  60.0 31.7 %collective-permute-done.20 = bf16[3,96,384]{2,1,0:T(8,128)(2,1)S(1)} collective-permute-done((bf16[3,96,384]{2,1,0:T(8,128)(2,1)S(1)}, bf16[3,96,384]{2,1,0:T(8,128)(2,1)S(1)}, u32[]{:S(2)}, u32[]{:S(2)}) %collective-permute-start.20) | collective-permute-done | bytes 221216 | tf_op jit(solution)/shard_map/ppermute | solution.py:14
  91.8 1.9 %collective-permute-start.21 = (bf16[3,96,384]{2,1,0:T(8,128)(2,1)S(1)}, bf16[3,96,384]{2,1,0:T(8,128)(2,1)}, u32[]{:S(2)}, u32[]{:S(2)}) collective-permute-start(bf16[3,96,384]{2,1,0:T(8,128)(2,1)S(1)} %broadcast_select_fusion.9), channel_id=1, source_target_pairs={{0,16},{1,17},{2,18},{3,19},{4,20},{5,21},{6,22},{7,23},{8,24},{9,... | collective-permute-start | bytes 663560 | tf_op jit(solution)/shard_map/ppermute | solution.py:14
  95.9 3.9 %collective-permute-start.2 = (bf16[384,768]{1,0:T(8,128)(2,1)S(1)}, bf16[384,768]{1,0:T(8,128)(2,1)S(1)}, u32[]{:S(2)}, u32[]{:S(2)}) collective-permute-start(bf16[384,768]{1,0:T(8,128)(2,1)S(1)} %collective-permute-done.1.b_above), channel_id=1, source_target_pairs={{1,17},{2,18},{3,19},{4,20},{5,21},{6,22},{7,23},{8,24},{9,25},{10... | collective-permute-start | bytes 1769480 | tf_op jit(solution)/shard_map/ppermute | solution.py:14
  101.0 1.9 %collective-permute-start.22 = (bf16[2,3,48,384]{3,2,1,0:T(8,128)(2,1)S(1)}, bf16[2,3,48,384]{3,2,1,0:T(8,128)(2,1)S(1)}, u32[]{:S(2)}, u32[]{:S(2)}) collective-permute-start(bf16[2,3,48,384]{3,2,1,0:T(8,128)(2,1)S(1)} %get-tuple-element.30), channel_id=1, source_target_pairs={{0,128},{1,129},{2,130},{3,131},{4,132},{5,133},{6,134},{7,135},{8... | collective-permute-start | bytes 663560 | tf_op jit(solution)/shard_map/ppermute | solution.py:14
  105.3 5.5 %collective-permute-start.24 = (bf16[2,3,48,384]{3,2,1,0:T(8,128)(2,1)S(1)}, bf16[2,3,48,384]{3,2,1,0:T(8,128)(2,1)S(1)}, u32[]{:S(2)}, u32[]{:S(2)}) collective-permute-start(bf16[2,3,48,384]{3,2,1,0:T(8,128)(2,1)S(1)} %get-tuple-element.29), channel_id=1, source_target_pairs={{0,384},{1,385},{2,386},{3,387},{4,388},{5,389},{6,390},{7,391},{8... | collective-permute-start | bytes 663560 | tf_op jit(solution)/shard_map/ppermute | solution.py:14
  110.8 7.9 %collective-permute-done.22 = bf16[2,3,48,384]{3,2,1,0:T(8,128)(2,1)S(1)} collective-permute-done((bf16[2,3,48,384]{3,2,1,0:T(8,128)(2,1)S(1)}, bf16[2,3,48,384]{3,2,1,0:T(8,128)(2,1)S(1)}, u32[]{:S(2)}, u32[]{:S(2)}) %collective-permute-start.22) | collective-permute-done | bytes 221216 | tf_op jit(solution)/shard_map/ppermute | solution.py:14
  118.8 1.9 %collective-permute-start.23 = (bf16[2,2,3,48,384]{4,3,2,1,0:T(8,128)(2,1)S(1)}, bf16[2,2,3,48,384]{4,3,2,1,0:T(8,128)(2,1)S(1)}, u32[]{:S(2)}, u32[]{:S(2)}) collective-permute-start(bf16[2,2,3,48,384]{4,3,2,1,0:T(8,128)(2,1)S(1)} %pad_maximum_fusion.p_one), channel_id=1, source_target_pairs={{0,384},{1,385},{2,386},{3,387},{4,388},{5,389},{6,390},{7,391},{8... | collective-permute-start | bytes 1327112 | tf_op jit(solution)/shard_map/ppermute | solution.py:14
  121.9 2.1 %collective-permute-start.29 = (bf16[2,384,384]{2,1,0:T(8,128)(2,1)S(1)}, bf16[2,384,384]{2,1,0:T(8,128)(2,1)S(1)}, u32[]{:S(2)}, u32[]{:S(2)}) collective-permute-start(bf16[2,384,384]{2,1,0:T(8,128)(2,1)S(1)} %broadcast_select_fusion.2.across), channel_id=1, source_target_pairs={{0,1},{2,3},{4,5},{6,7},{8,9},{10,11},{12,13},{14,15},{16,17},{18,... | collective-permute-start | bytes 1769480 | tf_op jit(solution)/shard_map/ppermute | solution.py:14
  124.1 1.9 %collective-permute-start.25 = (bf16[2,2,3,48,384]{4,3,2,1,0:T(8,128)(2,1)S(1)}, bf16[2,2,3,48,384]{4,3,2,1,0:T(8,128)(2,1)S(1)}, u32[]{:S(2)}, u32[]{:S(2)}) collective-permute-start(bf16[2,2,3,48,384]{4,3,2,1,0:T(8,128)(2,1)S(1)} %pad_maximum_fusion.1.q_one), channel_id=1, source_target_pairs={{0,128},{1,129},{2,130},{3,131},{4,132},{5,133},{6,134},{7,135},{8... | collective-permute-start | bytes 1327112 | tf_op jit(solution)/shard_map/ppermute | solution.py:14
  128.6 4.2 %collective-permute-done.23.p_two = bf16[2,2,3,48,384]{4,3,2,1,0:T(8,128)(2,1)S(1)} collective-permute-done((bf16[2,2,3,48,384]{4,3,2,1,0:T(8,128)(2,1)S(1)}, bf16[2,2,3,48,384]{4,3,2,1,0:T(8,128)(2,1)S(1)}, u32[]{:S(2)}, u32[]{:S(2)}) %collective-permute-start.23) | collective-permute-done | bytes 442400 | tf_op jit(solution)/shard_map/ppermute | solution.py:14
  132.8 4.6 %collective-permute-done.25.q_two = bf16[2,2,3,48,384]{4,3,2,1,0:T(8,128)(2,1)S(1)} collective-permute-done((bf16[2,2,3,48,384]{4,3,2,1,0:T(8,128)(2,1)S(1)}, bf16[2,2,3,48,384]{4,3,2,1,0:T(8,128)(2,1)S(1)}, u32[]{:S(2)}, u32[]{:S(2)}) %collective-permute-start.25) | collective-permute-done | bytes 442400 | tf_op jit(solution)/shard_map/ppermute | solution.py:14
  137.5 5.0 %shard_map.94 = f32[384,768]{1,0:T(8,128)} custom-call(s32[14]{0:T(128)S(1)} %stack.74.info, f32[384,768]{1,0:T(8,128)S(1)} %copy-done, bf16[384,768]{1,0:T(8,128)(2,1)S(1)} %copy-done.1, bf16[384,768]{1,0:T(8,128)(2,1)S(1)} %collective-permute-done.n, bf16[384,768]{1,0:T(8,128)(2,1)} %b.1, bf16[384,768]{1,0:T(8,128)(2,1)S(1)} %collective-permute-done.1.b_above, ...), custom_call_target="tpu_custom_call" | custom-call | flops 1358954496 | bytes 10616832 | tf_op jit(solution)/shard_map/pallas_call | solution.py:158
  (118 shorter events, 32.8 us)
Async XLA Ops:
  1.5 8.7 %collective-permute-start.7 = (bf16[384]{0:T(512)(128)(2,1)}, bf16[384]{0:T(512)(128)(2,1)S(1)}, u32[]{:S(2)}, u32[]{:S(2)}) collective-permute-start(bf16[384]{0:T(512)(128)(2,1)} %param.17), channel_id=1, source_target_pairs={{0,16},{16,32},{33,49},{49,65},{66,82},{82,98},{99,115},{115,131},... | collective-permute-start | bytes 2312 | tf_op jit(solution)/shard_map/ppermute | solution.py:14
  2.2 20.4 %collective-permute-start = (bf16[384,768]{1,0:T(8,128)(2,1)}, bf16[384,768]{1,0:T(8,128)(2,1)S(1)}, u32[]{:S(2)}, u32[]{:S(2)}) collective-permute-start(bf16[384,768]{1,0:T(8,128)(2,1)} %a.3), channel_id=1, source_target_pairs={{1,0},{2,1},{3,2},{4,3},{5,4},{6,5},{7,6},{8,7},{9,8},{10,9},{11,1... | collective-permute-start | bytes 1769480 | tf_op jit(solution)/shard_map/ppermute | solution.py:14
  4.2 7.0 %collective-permute-start.4 = (bf16[384,384]{1,0:T(8,128)(2,1)S(1)}, bf16[384,384]{1,0:T(8,128)(2,1)}, u32[]{:S(2)}, u32[]{:S(2)}) collective-permute-start(bf16[384,384]{1,0:T(8,128)(2,1)S(1)} %collective-permute-done.3.v), channel_id=1, source_target_pairs={{16,32},{32,48},{49,65},{65,81},{82,98},{98,114},{115,131},{131,14... | collective-permute-start | bytes 884744 | tf_op jit(solution)/shard_map/ppermute | solution.py:14
  8.9 12.2 %collective-permute-start.12 = (bf16[384,384]{1,0:T(8,128)(2,1)}, bf16[384,384]{1,0:T(8,128)(2,1)}, u32[]{:S(2)}, u32[]{:S(2)}) collective-permute-start(bf16[384,384]{1,0:T(8,128)(2,1)} %get-tuple-element.28), channel_id=1, source_target_pairs={{0,32},{17,49},{33,65},{50,82},{66,98},{83,115},{99,131},{116,148}... | collective-permute-start | bytes 884744 | tf_op jit(solution)/shard_map/ppermute | solution.py:14
  14.9 8.3 %collective-permute-start.11 = (bf16[384,384]{1,0:T(8,128)(2,1)}, bf16[384,384]{1,0:T(8,128)(2,1)S(1)}, u32[]{:S(2)}, u32[]{:S(2)}) collective-permute-start(bf16[384,384]{1,0:T(8,128)(2,1)} %get-tuple-element.15.own), channel_id=1, source_target_pairs={{32,16},{48,32},{65,49},{81,65},{98,82},{114,98},{131,115},{147,13... | collective-permute-start | bytes 884744 | tf_op jit(solution)/shard_map/ppermute | solution.py:14
  15.6 8.4 %collective-permute-start.10 = (bf16[384,384]{1,0:T(8,128)(2,1)}, bf16[384,384]{1,0:T(8,128)(2,1)S(1)}, u32[]{:S(2)}, u32[]{:S(2)}) collective-permute-start(bf16[384,384]{1,0:T(8,128)(2,1)} %get-tuple-element.15.own), channel_id=1, source_target_pairs={{32,33},{48,49},{65,66},{81,82},{98,99},{114,115},{131,132},{147,1... | collective-permute-start | bytes 884744 | tf_op jit(solution)/shard_map/ppermute | solution.py:14
  16.3 25.1 %collective-permute-start.1 = (bf16[384,768]{1,0:T(8,128)(2,1)}, bf16[384,768]{1,0:T(8,128)(2,1)S(1)}, u32[]{:S(2)}, u32[]{:S(2)}) collective-permute-start(bf16[384,768]{1,0:T(8,128)(2,1)} %b.1), channel_id=1, source_target_pairs={{0,16},{1,17},{2,18},{3,19},{4,20},{5,21},{6,22},{7,23},{8,24},{9,... | collective-permute-start | bytes 1769480 | tf_op jit(solution)/shard_map/ppermute | solution.py:14
  21.9 8.1 %collective-permute-start.15 = (bf16[384,384]{1,0:T(8,128)(2,1)S(1)}, bf16[384,384]{1,0:T(8,128)(2,1)S(1)}, u32[]{:S(2)}, u32[]{:S(2)}) collective-permute-start(bf16[384,384]{1,0:T(8,128)(2,1)S(1)} %copy-done.22), channel_id=1, source_target_pairs={{1,33},{17,49},{34,66},{50,82},{67,99},{83,115},{100,132},{116,148... | collective-permute-start | bytes 884744 | tf_op jit(solution)/shard_map/ppermute | solution.py:14
  22.6 18.8 %collective-permute-start.9 = (bf16[384,384]{1,0:T(8,128)(2,1)}, bf16[384,384]{1,0:T(8,128)(2,1)S(1)}, u32[]{:S(2)}, u32[]{:S(2)}) collective-permute-start(bf16[384,384]{1,0:T(8,128)(2,1)} %get-tuple-element.15.own), channel_id=1, source_target_pairs={{32,0},{48,16},{65,33},{81,49},{98,66},{114,82},{131,99},{147,115}... | collective-permute-start | bytes 884744 | tf_op jit(solution)/shard_map/ppermute | solution.py:14
  28.6 12.8 %collective-permute-start.14 = (bf16[384,384]{1,0:T(8,128)(2,1)S(1)}, bf16[384,384]{1,0:T(8,128)(2,1)S(1)}, u32[]{:S(2)}, u32[]{:S(2)}) collective-permute-start(bf16[384,384]{1,0:T(8,128)(2,1)S(1)} %get-tuple-element.16.own), channel_id=1, source_target_pairs={{32,33},{65,66},{98,99},{131,132},{164,165},{197,198},{230,231},{2... | collective-permute-start | bytes 884744 | tf_op jit(solution)/shard_map/ppermute | solution.py:14
  29.3 12.2 %collective-permute-start.13 = (bf16[384,384]{1,0:T(8,128)(2,1)S(1)}, bf16[384,384]{1,0:T(8,128)(2,1)S(1)}, u32[]{:S(2)}, u32[]{:S(2)}) collective-permute-start(bf16[384,384]{1,0:T(8,128)(2,1)S(1)} %get-tuple-element.16.own), channel_id=1, source_target_pairs={{16,0},{32,16},{49,33},{65,49},{82,66},{98,82},{115,99},{131,115},... | collective-permute-start | bytes 884744 | tf_op jit(solution)/shard_map/ppermute | solution.py:14
  46.6 8.0 %collective-permute-start.26 = (bf16[2,384,384]{2,1,0:T(8,128)(2,1)}, bf16[2,384,384]{2,1,0:T(8,128)(2,1)}, u32[]{:S(2)}, u32[]{:S(2)}) collective-permute-start(bf16[2,384,384]{2,1,0:T(8,128)(2,1)} %get-tuple-element.21), channel_id=1, source_target_pairs={{0,8},{16,24},{33,41},{49,57},{66,74},{82,90},{99,107},{115,123},{... | collective-permute-start | bytes 1769480 | tf_op jit(solution)/shard_map/ppermute | solution.py:14
  55.8 37.9 %collective-permute-start.27 = (bf16[2,384,384]{2,1,0:T(8,128)(2,1)S(1)}, bf16[2,384,384]{2,1,0:T(8,128)(2,1)S(1)}, u32[]{:S(2)}, u32[]{:S(2)}) collective-permute-start(bf16[2,384,384]{2,1,0:T(8,128)(2,1)S(1)} %broadcast_select_fusion), channel_id=1, source_target_pairs={{0,4},{8,12},{16,20},{24,28},{33,37},{41,45},{49,53},{57,61},{66,7... | collective-permute-start | bytes 1769480 | tf_op jit(solution)/shard_map/ppermute | solution.py:14
  56.5 35.2 %collective-permute-start.20 = (bf16[3,96,384]{2,1,0:T(8,128)(2,1)S(1)}, bf16[3,96,384]{2,1,0:T(8,128)(2,1)S(1)}, u32[]{:S(2)}, u32[]{:S(2)}) collective-permute-start(bf16[3,96,384]{2,1,0:T(8,128)(2,1)S(1)} %broadcast_select_fusion.8), channel_id=1, source_target_pairs={{0,32},{112,80},{128,160},{240,208},{256,288},{368,336},{384,416},... | collective-permute-start | bytes 663560 | tf_op jit(solution)/shard_map/ppermute | solution.py:14
  58.6 44.3 %collective-permute-start.31 = (bf16[1,384,384]{2,1,0:T(8,128)(2,1)}, bf16[1,384,384]{2,1,0:T(8,128)(2,1)}, u32[]{:S(2)}, u32[]{:S(2)}) collective-permute-start(bf16[1,384,384]{2,1,0:T(8,128)(2,1)} %broadcast_select_fusion.3), channel_id=1, source_target_pairs={{0,4},{8,12},{16,20},{24,28},{33,37},{41,45},{49,53},{57,61},{66,7... | collective-permute-start | bytes 884744 | tf_op jit(solution)/shard_map/ppermute | solution.py:14
  91.8 8.1 %collective-permute-start.21 = (bf16[3,96,384]{2,1,0:T(8,128)(2,1)S(1)}, bf16[3,96,384]{2,1,0:T(8,128)(2,1)}, u32[]{:S(2)}, u32[]{:S(2)}) collective-permute-start(bf16[3,96,384]{2,1,0:T(8,128)(2,1)S(1)} %broadcast_select_fusion.9), channel_id=1, source_target_pairs={{0,16},{1,17},{2,18},{3,19},{4,20},{5,21},{6,22},{7,23},{8,24},{9,... | collective-permute-start | bytes 663560 | tf_op jit(solution)/shard_map/ppermute | solution.py:14
  94.6 26.1 %collective-permute-start.28 = (bf16[2,384,384]{2,1,0:T(8,128)(2,1)}, bf16[2,384,384]{2,1,0:T(8,128)(2,1)}, u32[]{:S(2)}, u32[]{:S(2)}) collective-permute-start(bf16[2,384,384]{2,1,0:T(8,128)(2,1)} %broadcast_select_fusion.1), channel_id=1, source_target_pairs={{0,2},{4,6},{8,10},{12,14},{16,18},{20,22},{24,26},{28,30},{33,35}... | collective-permute-start | bytes 1769480 | tf_op jit(solution)/shard_map/ppermute | solution.py:14
  95.9 31.5 %collective-permute-start.2 = (bf16[384,768]{1,0:T(8,128)(2,1)S(1)}, bf16[384,768]{1,0:T(8,128)(2,1)S(1)}, u32[]{:S(2)}, u32[]{:S(2)}) collective-permute-start(bf16[384,768]{1,0:T(8,128)(2,1)S(1)} %collective-permute-done.1.b_above), channel_id=1, source_target_pairs={{1,17},{2,18},{3,19},{4,20},{5,21},{6,22},{7,23},{8,24},{9,25},{10... | collective-permute-start | bytes 1769480 | tf_op jit(solution)/shard_map/ppermute | solution.py:14
  101.0 17.8 %collective-permute-start.22 = (bf16[2,3,48,384]{3,2,1,0:T(8,128)(2,1)S(1)}, bf16[2,3,48,384]{3,2,1,0:T(8,128)(2,1)S(1)}, u32[]{:S(2)}, u32[]{:S(2)}) collective-permute-start(bf16[2,3,48,384]{3,2,1,0:T(8,128)(2,1)S(1)} %get-tuple-element.30), channel_id=1, source_target_pairs={{0,128},{1,129},{2,130},{3,131},{4,132},{5,133},{6,134},{7,135},{8... | collective-permute-start | bytes 663560 | tf_op jit(solution)/shard_map/ppermute | solution.py:14
  104.0 22.1 %collective-permute-start.32 = (bf16[1,384,384]{2,1,0:T(8,128)(2,1)S(1)}, bf16[1,384,384]{2,1,0:T(8,128)(2,1)S(1)}, u32[]{:S(2)}, u32[]{:S(2)}) collective-permute-start(bf16[1,384,384]{2,1,0:T(8,128)(2,1)S(1)} %broadcast_select_fusion.4), channel_id=1, source_target_pairs={{0,2},{4,6},{8,10},{12,14},{16,18},{20,22},{24,26},{28,30},{33,35}... | collective-permute-start | bytes 884744 | tf_op jit(solution)/shard_map/ppermute | solution.py:14
  105.3 18.8 %collective-permute-start.24 = (bf16[2,3,48,384]{3,2,1,0:T(8,128)(2,1)S(1)}, bf16[2,3,48,384]{3,2,1,0:T(8,128)(2,1)S(1)}, u32[]{:S(2)}, u32[]{:S(2)}) collective-permute-start(bf16[2,3,48,384]{3,2,1,0:T(8,128)(2,1)S(1)} %get-tuple-element.29), channel_id=1, source_target_pairs={{0,384},{1,385},{2,386},{3,387},{4,388},{5,389},{6,390},{7,391},{8... | collective-permute-start | bytes 663560 | tf_op jit(solution)/shard_map/ppermute | solution.py:14
  118.8 14.0 %collective-permute-start.23 = (bf16[2,2,3,48,384]{4,3,2,1,0:T(8,128)(2,1)S(1)}, bf16[2,2,3,48,384]{4,3,2,1,0:T(8,128)(2,1)S(1)}, u32[]{:S(2)}, u32[]{:S(2)}) collective-permute-start(bf16[2,2,3,48,384]{4,3,2,1,0:T(8,128)(2,1)S(1)} %pad_maximum_fusion.p_one), channel_id=1, source_target_pairs={{0,384},{1,385},{2,386},{3,387},{4,388},{5,389},{6,390},{7,391},{8... | collective-permute-start | bytes 1327112 | tf_op jit(solution)/shard_map/ppermute | solution.py:14
  121.9 15.5 %collective-permute-start.29 = (bf16[2,384,384]{2,1,0:T(8,128)(2,1)S(1)}, bf16[2,384,384]{2,1,0:T(8,128)(2,1)S(1)}, u32[]{:S(2)}, u32[]{:S(2)}) collective-permute-start(bf16[2,384,384]{2,1,0:T(8,128)(2,1)S(1)} %broadcast_select_fusion.2.across), channel_id=1, source_target_pairs={{0,1},{2,3},{4,5},{6,7},{8,9},{10,11},{12,13},{14,15},{16,17},{18,... | collective-permute-start | bytes 1769480 | tf_op jit(solution)/shard_map/ppermute | solution.py:14
  124.1 13.3 %collective-permute-start.25 = (bf16[2,2,3,48,384]{4,3,2,1,0:T(8,128)(2,1)S(1)}, bf16[2,2,3,48,384]{4,3,2,1,0:T(8,128)(2,1)S(1)}, u32[]{:S(2)}, u32[]{:S(2)}) collective-permute-start(bf16[2,2,3,48,384]{4,3,2,1,0:T(8,128)(2,1)S(1)} %pad_maximum_fusion.1.q_one), channel_id=1, source_target_pairs={{0,128},{1,129},{2,130},{3,131},{4,132},{5,133},{6,134},{7,135},{8... | collective-permute-start | bytes 1327112 | tf_op jit(solution)/shard_map/ppermute | solution.py:14
  (35 other events, 225.9 us)

commit v4 on v3

--- a/solution.py
+++ b/solution.py
@@ -64,7 +64,7 @@
 
 
 def third_wave(
-    info, c, a, n, col_two, row_two, col_one, row_one, own, b_two, b_above, u, p, lam, v, q, mu,
+    info, c, a, n, col_two, row_two, col_one, row_one, own, b_two, b_one, u, p, lam, v, q, mu,
     x, *parts,
 ):
     slot = info[2]
@@ -76,7 +76,7 @@
         - dot(tile_of(n, slot), col_two[...])
         - dot(row_two[...], b_two[...])
         - dot(a_tile, col_one[...])
-        - dot(left, tile_of(b_above, slot))
+        - dot(left, b_one[...])
     )
     value = solve(residue, (u, p, lam), (v, q, mu))
     x[...] = value
@@ -267,16 +267,19 @@
         )
     ]
     b_tiles = b_upper[:, :tile], b_upper[:, tile:]
-    b_wave = send(jnp.where(d == -1, *b_tiles), band((-1, 0), 2, 0))
-    b_two = send(jnp.where(d == -2, *b_tiles), band((-2, -1), 2, 0))
+    near = jnp.where(d == -1, *b_tiles)
+    far = jnp.where(d == -2, *b_tiles)
+    b_wave = send(near, band((-1, 0), 2, 0))
+    b_one = send(near, band((-1, 0), 1, 0))
+    b_two = send(far, band((-2, -1), 2, 0))
     a_next = send(a_upper, [((r, c), (r, c - 1)) for r in range(ROWS) for c in range(1, COLS)])
 
-    def rows_down(last):
+    def rows_down():
         rows = range(ROWS - 1)
-        return [((r, c), (r + 1, c)) for r in rows for c in range(COLS) if r + 1 <= 2 * c + last]
-
-    b_above = send(b_upper, rows_down(1))
-    b_above_two = send(b_above, rows_down(0))
+        return [((r, c), (r + 1, c)) for r in rows for c in range(COLS) if r + 1 <= 2 * c]
+
+    b_above = send(b_upper, rows_down())
+    b_above_two = send(b_above, rows_down())
 
     x_two, solved_two = run(
         "K2", first_wave, (exact, square), 4, None,
@@ -296,7 +299,7 @@
     x_zero, *quarters, across = run(
         "K0", third_wave, (exact, *[strip] * 4, pair), 8, info,
         c_zero, a_upper, a_next, col_two, row_two, col_one, row_one, solved_one,
-        b_two, b_above, *left, *rights[0],
+        b_two, b_one, *left, *rights[0],
     )
     pieces = col_spread(quarters, row, col)
     across, flipped = row_tree(across, offset)

time: 144 us -> 143 us (level)
  the two profiles are of different devices: /device:TPU:26 before, /device:TPU:40 now
where the time goes in v4:
time: 143 us; the launch traced here: 142 us
  waiting for transfers between devices  56.7 us (40%)
  starting transfers between devices  53.4 us (37%)
  Pallas kernels  14.8 us (10%)
  other arithmetic  9.28 us (6%)
  local copies, waits for them, and re-layouts  7.05 us (5%)
    ppermute x35, waiting for transfers between devices, send(): return lax.ppermute(x, ('row', 'col'), flat)  56.7 us
    ppermute x35, starting transfers between devices, send(): return lax.ppermute(x, ('row', 'col'), flat)  53.4 us
    pallas_call x4, Pallas kernels, run(): pl.pallas_call(kernel, out_shape=outs, in_specs=[pl.BlockSpec(memory_spac...  14.8 us
    unnamed x56, local copies, waits for them, and re-layouts  6.72 us
    select_n x6, other arithmetic, row_tree(): x = jnp.where(takes, got, x)  5.02 us
  transfers between devices with their start and end apart: 35, of which 5 were waited for; matrix products, arithmetic and copies ran while one was open for 7% of the time, Pallas kernels for 4%

profile of v4, /device:TPU:40, one launch (start us, length us, event | category | flops | bytes accessed | tf_op | source)
XLA Modules:
  0.0 142.0 jit_solution(16297312252279128776)
XLA Ops:
  2.2 2.7 %collective-permute-start = (bf16[384,768]{1,0:T(8,128)(2,1)}, bf16[384,768]{1,0:T(8,128)(2,1)S(1)}, u32[]{:S(2)}, u32[]{:S(2)}) collective-permute-start(bf16[384,768]{1,0:T(8,128)(2,1)} %a.3), channel_id=1, source_target_pairs={{1,0},{2,1},{3,2},{4,3},{5,4},{6,5},{7,6},{8,7},{9,8},{10,9},{11,1... | collective-permute-start | bytes 1769480 | tf_op jit(solution)/shard_map/ppermute | solution.py:14
  4.9 1.4 collective-permute-start.4
  6.3 1.4 collective-permute-start.6
  7.7 2.0 %broadcast_select_fusion.6 = (bf16[384,384]{1,0:T(8,128)(2,1)}, bf16[384,384]{1,0:T(8,128)(2,1)}) fusion(pred[]{:T(512)S(6)} %eq.65, bf16[384,768]{1,0:T(8,128)(2,1)} %b.1, pred[]{:T(512)S(6)} %eq.64), kind=kLoop, calls=%fused_computation.11 | loop fusion | flops 294912 | bytes 1179650 | tf_op jit(solution)/shard_map/jit(_where)/select_n | solution.py:271
  11.3 2.9 %shard_map.91 = (f32[384,384]{1,0:T(8,128)S(1)}, bf16[384,384]{1,0:T(8,128)(2,1)}) custom-call(bf16[384,384]{1,0:T(8,128)(2,1)S(1)} %dynamic-slice_convert_fusion.c, bf16[384,384]{1,0:T(8,128)(2,1)S(1)} %copy-done.3, bf16[384,384]{1,0:T(8,128)(2,1)S(1)} %copy-done.5, f32[384,1]{1,0:T(8,128)S(1)} %reshape.4.lam, bf16[384,384]{1,0:T(8,128)(2,1)} %collective-permute-done.4.v, ...), custom_call_target="tpu_custom_call" | custom-call | flops 452984832 | bytes 2362368 | tf_op jit(solution)/shard_map/pallas_call | solution.py:158
  16.4 1.4 collective-permute-start.16
  22.9 2.7 %shard_map.92 = (f32[384,384]{1,0:T(8,128)S(1)}, bf16[384,384]{1,0:T(8,128)(2,1)S(1)}) custom-call(s32[14]{0:T(128)S(1)} %stack.74.info, f32[384,384]{1,0:T(8,128)S(1)} %get-tuple-element.25.c, bf16[384,768]{1,0:T(8,128)(2,1)S(1)} %collective-permute-done.n, bf16[384,384]{1,0:T(8,128)(2,1)S(1)} %copy-done.22, ...), custom_call_target="tpu_custom_call" | custom-call | flops 679477248 | bytes 4426752 | tf_op jit(solution)/shard_map/pallas_call | solution.py:158
  28.0 4.1 %shard_map.93 = (f32[384,384]{1,0:T(8,128)S(1)}, bf16[3,96,384]{2,1,0:T(8,128)(2,1)S(1)}, bf16[3,96,384]{2,1,0:T(8,128)(2,1)}, bf16[3,96,384]{2,1,0:T(8,128)(2,1...) custom-call(s32[14]{0:T(128)S(1)} %stack.74.info, f32[384,384]{1,0:T(8,128)S(1)} %get-tuple-element.26.c, ...), custom_call_target="tpu_custom_call" | custom-call | flops 905969664 | bytes 7080960 | tf_op jit(solution)/shard_map/pallas_call | solution.py:158
  33.7 1.5 %collective-permute-start.27 = (bf16[2,384,384]{2,1,0:T(8,128)(2,1)}, bf16[2,384,384]{2,1,0:T(8,128)(2,1)}, u32[]{:S(2)}, u32[]{:S(2)}) collective-permute-start(bf16[2,384,384]{2,1,0:T(8,128)(2,1)} %get-tuple-element.21), channel_id=1, source_target_pairs={{0,8},{16,24},{33,41},{49,57},{66,74},{82,90},{99,107},{115,123},{... | collective-permute-start | bytes 1769480 | tf_op jit(solution)/shard_map/ppermute | solution.py:14
  35.1 1.4 collective-permute-start.17
  39.2 5.1 %collective-permute-start.1 = (bf16[384,768]{1,0:T(8,128)(2,1)S(1)}, bf16[384,768]{1,0:T(8,128)(2,1)}, u32[]{:S(2)}, u32[]{:S(2)}) collective-permute-start(bf16[384,768]{1,0:T(8,128)(2,1)S(1)} %copy-done.2), channel_id=1, source_target_pairs={{1,17},{2,18},{3,19},{4,20},{5,21},{6,22},{7,23},{8,24},{9,25},{10... | collective-permute-start | bytes 1769480 | tf_op jit(solution)/shard_map/ppermute | solution.py:14
  50.7 1.4 collective-permute-start.32
  52.0 44.7 %collective-permute-done.21 = bf16[3,96,384]{2,1,0:T(8,128)(2,1)S(1)} collective-permute-done((bf16[3,96,384]{2,1,0:T(8,128)(2,1)S(1)}, bf16[3,96,384]{2,1,0:T(8,128)(2,1)S(1)}, u32[]{:S(2)}, u32[]{:S(2)}) %collective-permute-start.21) | collective-permute-done | bytes 221216 | tf_op jit(solution)/shard_map/ppermute | solution.py:14
  96.8 1.9 %collective-permute-start.22 = (bf16[3,96,384]{2,1,0:T(8,128)(2,1)S(1)}, bf16[3,96,384]{2,1,0:T(8,128)(2,1)}, u32[]{:S(2)}, u32[]{:S(2)}) collective-permute-start(bf16[3,96,384]{2,1,0:T(8,128)(2,1)S(1)} %broadcast_select_fusion.9), channel_id=1, source_target_pairs={{0,16},{1,17},{2,18},{3,19},{4,20},{5,21},{6,22},{7,23},{8,24},{9,... | collective-permute-start | bytes 663560 | tf_op jit(solution)/shard_map/ppermute | solution.py:14
  101.0 4.0 %collective-permute-start.2 = (bf16[384,768]{1,0:T(8,128)(2,1)}, bf16[384,768]{1,0:T(8,128)(2,1)S(1)}, u32[]{:S(2)}, u32[]{:S(2)}) collective-permute-start(bf16[384,768]{1,0:T(8,128)(2,1)} %collective-permute-done.1.b_above), channel_id=1, source_target_pairs={{1,17},{2,18},{3,19},{4,20},{5,21},{6,22},{7,23},{8,24},{9,25},{10... | collective-permute-start | bytes 1769480 | tf_op jit(solution)/shard_map/ppermute | solution.py:14
  106.1 1.9 %collective-permute-start.25 = (bf16[2,3,48,384]{3,2,1,0:T(8,128)(2,1)S(1)}, bf16[2,3,48,384]{3,2,1,0:T(8,128)(2,1)S(1)}, u32[]{:S(2)}, u32[]{:S(2)}) collective-permute-start(bf16[2,3,48,384]{3,2,1,0:T(8,128)(2,1)S(1)} %get-tuple-element.29), channel_id=1, source_target_pairs={{0,384},{1,385},{2,386},{3,387},{4,388},{5,389},{6,390},{7,391},{8... | collective-permute-start | bytes 663560 | tf_op jit(solution)/shard_map/ppermute | solution.py:14
  110.3 1.9 %collective-permute-start.23 = (bf16[2,3,48,384]{3,2,1,0:T(8,128)(2,1)S(1)}, bf16[2,3,48,384]{3,2,1,0:T(8,128)(2,1)S(1)}, u32[]{:S(2)}, u32[]{:S(2)}) collective-permute-start(bf16[2,3,48,384]{3,2,1,0:T(8,128)(2,1)S(1)} %get-tuple-element.30), channel_id=1, source_target_pairs={{0,128},{1,129},{2,130},{3,131},{4,132},{5,133},{6,134},{7,135},{8... | collective-permute-start | bytes 663560 | tf_op jit(solution)/shard_map/ppermute | solution.py:14
  112.2 2.9 %collective-permute-done.25 = bf16[2,3,48,384]{3,2,1,0:T(8,128)(2,1)S(1)} collective-permute-done((bf16[2,3,48,384]{3,2,1,0:T(8,128)(2,1)S(1)}, bf16[2,3,48,384]{3,2,1,0:T(8,128)(2,1)S(1)}, u32[]{:S(2)}, u32[]{:S(2)}) %collective-permute-start.25) | collective-permute-done | bytes 221216 | tf_op jit(solution)/shard_map/ppermute | solution.py:14
  115.1 4.2 %collective-permute-start.26 = (bf16[2,2,3,48,384]{4,3,2,1,0:T(8,128)(2,1)S(1)}, bf16[2,2,3,48,384]{4,3,2,1,0:T(8,128)(2,1)S(1)}, u32[]{:S(2)}, u32[]{:S(2)}) collective-permute-start(bf16[2,2,3,48,384]{4,3,2,1,0:T(8,128)(2,1)S(1)} %pad_maximum_fusion.1.q_one), channel_id=1, source_target_pairs={{0,128},{1,129},{2,130},{3,131},{4,132},{5,133},{6,134},{7,135},{8... | collective-permute-start | bytes 1327112 | tf_op jit(solution)/shard_map/ppermute | solution.py:14
  120.5 1.8 %collective-permute-start.30 = (bf16[2,384,384]{2,1,0:T(8,128)(2,1)S(1)}, bf16[2,384,384]{2,1,0:T(8,128)(2,1)S(1)}, u32[]{:S(2)}, u32[]{:S(2)}) collective-permute-start(bf16[2,384,384]{2,1,0:T(8,128)(2,1)S(1)} %broadcast_select_fusion.2.across), channel_id=1, source_target_pairs={{0,1},{2,3},{4,5},{6,7},{8,9},{10,11},{12,13},{14,15},{16,17},{18,... | collective-permute-start | bytes 1769480 | tf_op jit(solution)/shard_map/ppermute | solution.py:14
  122.4 4.0 %collective-permute-start.24 = (bf16[2,2,3,48,384]{4,3,2,1,0:T(8,128)(2,1)S(1)}, bf16[2,2,3,48,384]{4,3,2,1,0:T(8,128)(2,1)S(1)}, u32[]{:S(2)}, u32[]{:S(2)}) collective-permute-start(bf16[2,2,3,48,384]{4,3,2,1,0:T(8,128)(2,1)S(1)} %pad_maximum_fusion.p_one), channel_id=1, source_target_pairs={{0,384},{1,385},{2,386},{3,387},{4,388},{5,389},{6,390},{7,391},{8... | collective-permute-start | bytes 1327112 | tf_op jit(solution)/shard_map/ppermute | solution.py:14
  126.5 1.4 collective-permute-start.34
  129.7 7.3 %collective-permute-done.24.p_two = bf16[2,2,3,48,384]{4,3,2,1,0:T(8,128)(2,1)S(1)} collective-permute-done((bf16[2,2,3,48,384]{4,3,2,1,0:T(8,128)(2,1)S(1)}, bf16[2,2,3,48,384]{4,3,2,1,0:T(8,128)(2,1)S(1)}, u32[]{:S(2)}, u32[]{:S(2)}) %collective-permute-start.24) | collective-permute-done | bytes 442400 | tf_op jit(solution)/shard_map/ppermute | solution.py:14
  137.0 5.0 %shard_map.94 = f32[384,768]{1,0:T(8,128)} custom-call(s32[14]{0:T(128)S(1)} %stack.74.info, f32[384,768]{1,0:T(8,128)S(1)} %copy-done, bf16[384,768]{1,0:T(8,128)(2,1)S(1)} %copy-done.1, bf16[384,768]{1,0:T(8,128)(2,1)S(1)} %collective-permute-done.n, bf16[384,768]{1,0:T(8,128)(2,1)S(1)} %copy-done.2, bf16[384,768]{1,0:T(8,128)(2,1)} %collective-permute-done.1.b_above, ...), custom_call_target="tpu_custom_call" | custom-call | flops 1358954496 | bytes 10616832 | tf_op jit(solution)/shard_map/pallas_call | solution.py:158
  (126 shorter events, 32.3 us)
Async XLA Ops:
  1.5 8.8 %collective-permute-start.7 = (bf16[384]{0:T(512)(128)(2,1)}, bf16[384]{0:T(512)(128)(2,1)S(1)}, u32[]{:S(2)}, u32[]{:S(2)}) collective-permute-start(bf16[384]{0:T(512)(128)(2,1)} %param.17), channel_id=1, source_target_pairs={{0,16},{16,32},{33,49},{49,65},{66,82},{82,98},{99,115},{115,131},... | collective-permute-start | bytes 2312 | tf_op jit(solution)/shard_map/ppermute | solution.py:14
  2.2 17.3 %collective-permute-start = (bf16[384,768]{1,0:T(8,128)(2,1)}, bf16[384,768]{1,0:T(8,128)(2,1)S(1)}, u32[]{:S(2)}, u32[]{:S(2)}) collective-permute-start(bf16[384,768]{1,0:T(8,128)(2,1)} %a.3), channel_id=1, source_target_pairs={{1,0},{2,1},{3,2},{4,3},{5,4},{6,5},{7,6},{8,7},{9,8},{10,9},{11,1... | collective-permute-start | bytes 1769480 | tf_op jit(solution)/shard_map/ppermute | solution.py:14
  4.9 6.3 %collective-permute-start.4 = (bf16[384,384]{1,0:T(8,128)(2,1)S(1)}, bf16[384,384]{1,0:T(8,128)(2,1)}, u32[]{:S(2)}, u32[]{:S(2)}) collective-permute-start(bf16[384,384]{1,0:T(8,128)(2,1)S(1)} %collective-permute-done.3.v), channel_id=1, source_target_pairs={{16,32},{32,48},{49,65},{65,81},{82,98},{98,114},{115,131},{131,14... | collective-permute-start | bytes 884744 | tf_op jit(solution)/shard_map/ppermute | solution.py:14
  9.7 8.4 %collective-permute-start.12 = (bf16[384,384]{1,0:T(8,128)(2,1)}, bf16[384,384]{1,0:T(8,128)(2,1)S(1)}, u32[]{:S(2)}, u32[]{:S(2)}) collective-permute-start(bf16[384,384]{1,0:T(8,128)(2,1)} %get-tuple-element.28), channel_id=1, source_target_pairs={{0,32},{17,49},{33,65},{50,82},{66,98},{83,115},{99,131},{116,148}... | collective-permute-start | bytes 884744 | tf_op jit(solution)/shard_map/ppermute | solution.py:14
  16.4 11.5 %collective-permute-start.16 = (bf16[384,384]{1,0:T(8,128)(2,1)}, bf16[384,384]{1,0:T(8,128)(2,1)}, u32[]{:S(2)}, u32[]{:S(2)}) collective-permute-start(bf16[384,384]{1,0:T(8,128)(2,1)} %get-tuple-element.28), channel_id=1, source_target_pairs={{0,16},{17,33},{33,49},{50,66},{66,82},{83,99},{99,115},{116,132},... | collective-permute-start | bytes 884744 | tf_op jit(solution)/shard_map/ppermute | solution.py:14
  18.9 9.1 %collective-permute-start.15 = (bf16[384,384]{1,0:T(8,128)(2,1)S(1)}, bf16[384,384]{1,0:T(8,128)(2,1)S(1)}, u32[]{:S(2)}, u32[]{:S(2)}) collective-permute-start(bf16[384,384]{1,0:T(8,128)(2,1)S(1)} %copy-done.25), channel_id=1, source_target_pairs={{1,33},{17,49},{34,66},{50,82},{67,99},{83,115},{100,132},{116,148... | collective-permute-start | bytes 884744 | tf_op jit(solution)/shard_map/ppermute | solution.py:14
  19.5 8.4 %collective-permute-start.9 = (bf16[384,384]{1,0:T(8,128)(2,1)}, bf16[384,384]{1,0:T(8,128)(2,1)S(1)}, u32[]{:S(2)}, u32[]{:S(2)}) collective-permute-start(bf16[384,384]{1,0:T(8,128)(2,1)} %get-tuple-element.15.own), channel_id=1, source_target_pairs={{32,0},{48,16},{65,33},{81,49},{98,66},{114,82},{131,99},{147,115}... | collective-permute-start | bytes 884744 | tf_op jit(solution)/shard_map/ppermute | solution.py:14
  33.7 13.0 %collective-permute-start.27 = (bf16[2,384,384]{2,1,0:T(8,128)(2,1)}, bf16[2,384,384]{2,1,0:T(8,128)(2,1)}, u32[]{:S(2)}, u32[]{:S(2)}) collective-permute-start(bf16[2,384,384]{2,1,0:T(8,128)(2,1)} %get-tuple-element.21), channel_id=1, source_target_pairs={{0,8},{16,24},{33,41},{49,57},{66,74},{82,90},{99,107},{115,123},{... | collective-permute-start | bytes 1769480 | tf_op jit(solution)/shard_map/ppermute | solution.py:14
  35.1 9.2 %collective-permute-start.17 = (bf16[3,96,384]{2,1,0:T(8,128)(2,1)}, bf16[3,96,384]{2,1,0:T(8,128)(2,1)}, u32[]{:S(2)}, u32[]{:S(2)}) collective-permute-start(bf16[3,96,384]{2,1,0:T(8,128)(2,1)} %get-tuple-element.18), channel_id=1, source_target_pairs={{0,128},{16,144},{33,161},{49,177},{66,194},{82,210},{99,227},{115... | collective-permute-start | bytes 663560 | tf_op jit(solution)/shard_map/ppermute | solution.py:14
  36.5 8.5 %collective-permute-start.18 = (bf16[3,96,384]{2,1,0:T(8,128)(2,1)}, bf16[3,96,384]{2,1,0:T(8,128)(2,1)}, u32[]{:S(2)}, u32[]{:S(2)}) collective-permute-start(bf16[3,96,384]{2,1,0:T(8,128)(2,1)} %get-tuple-element.19), channel_id=1, source_target_pairs={{0,384},{16,400},{33,417},{49,433},{66,450},{82,466},{99,483},{115... | collective-permute-start | bytes 663560 | tf_op jit(solution)/shard_map/ppermute | solution.py:14
  37.8 7.2 %collective-permute-start.19 = (bf16[3,96,384]{2,1,0:T(8,128)(2,1)}, bf16[3,96,384]{2,1,0:T(8,128)(2,1)}, u32[]{:S(2)}, u32[]{:S(2)}) collective-permute-start(bf16[3,96,384]{2,1,0:T(8,128)(2,1)} %get-tuple-element.20), channel_id=1, source_target_pairs={{0,256},{16,272},{33,289},{49,305},{66,322},{82,338},{99,355},{115... | collective-permute-start | bytes 663560 | tf_op jit(solution)/shard_map/ppermute | solution.py:14
  39.2 61.7 %collective-permute-start.1 = (bf16[384,768]{1,0:T(8,128)(2,1)S(1)}, bf16[384,768]{1,0:T(8,128)(2,1)}, u32[]{:S(2)}, u32[]{:S(2)}) collective-permute-start(bf16[384,768]{1,0:T(8,128)(2,1)S(1)} %copy-done.2), channel_id=1, source_target_pairs={{1,17},{2,18},{3,19},{4,20},{5,21},{6,22},{7,23},{8,24},{9,25},{10... | collective-permute-start | bytes 1769480 | tf_op jit(solution)/shard_map/ppermute | solution.py:14
  47.9 50.9 %collective-permute-start.28 = (bf16[2,384,384]{2,1,0:T(8,128)(2,1)S(1)}, bf16[2,384,384]{2,1,0:T(8,128)(2,1)S(1)}, u32[]{:S(2)}, u32[]{:S(2)}) collective-permute-start(bf16[2,384,384]{2,1,0:T(8,128)(2,1)S(1)} %broadcast_select_fusion), channel_id=1, source_target_pairs={{0,4},{8,12},{16,20},{24,28},{33,37},{41,45},{49,53},{57,61},{66,7... | collective-permute-start | bytes 1769480 | tf_op jit(solution)/shard_map/ppermute | solution.py:14
  48.6 48.1 %collective-permute-start.21 = (bf16[3,96,384]{2,1,0:T(8,128)(2,1)S(1)}, bf16[3,96,384]{2,1,0:T(8,128)(2,1)S(1)}, u32[]{:S(2)}, u32[]{:S(2)}) collective-permute-start(bf16[3,96,384]{2,1,0:T(8,128)(2,1)S(1)} %broadcast_select_fusion.8), channel_id=1, source_target_pairs={{0,32},{112,80},{128,160},{240,208},{256,288},{368,336},{384,416},... | collective-permute-start | bytes 663560 | tf_op jit(solution)/shard_map/ppermute | solution.py:14
  50.7 57.3 %collective-permute-start.32 = (bf16[1,384,384]{2,1,0:T(8,128)(2,1)}, bf16[1,384,384]{2,1,0:T(8,128)(2,1)}, u32[]{:S(2)}, u32[]{:S(2)}) collective-permute-start(bf16[1,384,384]{2,1,0:T(8,128)(2,1)} %broadcast_select_fusion.3), channel_id=1, source_target_pairs={{0,4},{8,12},{16,20},{24,28},{33,37},{41,45},{49,53},{57,61},{66,7... | collective-permute-start | bytes 884744 | tf_op jit(solution)/shard_map/ppermute | solution.py:14
  96.8 8.1 %collective-permute-start.22 = (bf16[3,96,384]{2,1,0:T(8,128)(2,1)S(1)}, bf16[3,96,384]{2,1,0:T(8,128)(2,1)}, u32[]{:S(2)}, u32[]{:S(2)}) collective-permute-start(bf16[3,96,384]{2,1,0:T(8,128)(2,1)S(1)} %broadcast_select_fusion.9), channel_id=1, source_target_pairs={{0,16},{1,17},{2,18},{3,19},{4,20},{5,21},{6,22},{7,23},{8,24},{9,... | collective-permute-start | bytes 663560 | tf_op jit(solution)/shard_map/ppermute | solution.py:14
  99.6 19.7 %collective-permute-start.29 = (bf16[2,384,384]{2,1,0:T(8,128)(2,1)}, bf16[2,384,384]{2,1,0:T(8,128)(2,1)}, u32[]{:S(2)}, u32[]{:S(2)}) collective-permute-start(bf16[2,384,384]{2,1,0:T(8,128)(2,1)} %broadcast_select_fusion.1), channel_id=1, source_target_pairs={{0,2},{4,6},{8,10},{12,14},{16,18},{20,22},{24,26},{28,30},{33,35}... | collective-permute-start | bytes 1769480 | tf_op jit(solution)/shard_map/ppermute | solution.py:14
  101.0 26.9 %collective-permute-start.2 = (bf16[384,768]{1,0:T(8,128)(2,1)}, bf16[384,768]{1,0:T(8,128)(2,1)S(1)}, u32[]{:S(2)}, u32[]{:S(2)}) collective-permute-start(bf16[384,768]{1,0:T(8,128)(2,1)} %collective-permute-done.1.b_above), channel_id=1, source_target_pairs={{1,17},{2,18},{3,19},{4,20},{5,21},{6,22},{7,23},{8,24},{9,25},{10... | collective-permute-start | bytes 1769480 | tf_op jit(solution)/shard_map/ppermute | solution.py:14
  106.1 9.0 %collective-permute-start.25 = (bf16[2,3,48,384]{3,2,1,0:T(8,128)(2,1)S(1)}, bf16[2,3,48,384]{3,2,1,0:T(8,128)(2,1)S(1)}, u32[]{:S(2)}, u32[]{:S(2)}) collective-permute-start(bf16[2,3,48,384]{3,2,1,0:T(8,128)(2,1)S(1)} %get-tuple-element.29), channel_id=1, source_target_pairs={{0,384},{1,385},{2,386},{3,387},{4,388},{5,389},{6,390},{7,391},{8... | collective-permute-start | bytes 663560 | tf_op jit(solution)/shard_map/ppermute | solution.py:14
  109.0 17.4 %collective-permute-start.33 = (bf16[1,384,384]{2,1,0:T(8,128)(2,1)S(1)}, bf16[1,384,384]{2,1,0:T(8,128)(2,1)S(1)}, u32[]{:S(2)}, u32[]{:S(2)}) collective-permute-start(bf16[1,384,384]{2,1,0:T(8,128)(2,1)S(1)} %broadcast_select_fusion.4), channel_id=1, source_target_pairs={{0,2},{4,6},{8,10},{12,14},{16,18},{20,22},{24,26},{28,30},{33,35}... | collective-permute-start | bytes 884744 | tf_op jit(solution)/shard_map/ppermute | solution.py:14
  110.3 12.0 %collective-permute-start.23 = (bf16[2,3,48,384]{3,2,1,0:T(8,128)(2,1)S(1)}, bf16[2,3,48,384]{3,2,1,0:T(8,128)(2,1)S(1)}, u32[]{:S(2)}, u32[]{:S(2)}) collective-permute-start(bf16[2,3,48,384]{3,2,1,0:T(8,128)(2,1)S(1)} %get-tuple-element.30), channel_id=1, source_target_pairs={{0,128},{1,129},{2,130},{3,131},{4,132},{5,133},{6,134},{7,135},{8... | collective-permute-start | bytes 663560 | tf_op jit(solution)/shard_map/ppermute | solution.py:14
  115.1 14.5 %collective-permute-start.26 = (bf16[2,2,3,48,384]{4,3,2,1,0:T(8,128)(2,1)S(1)}, bf16[2,2,3,48,384]{4,3,2,1,0:T(8,128)(2,1)S(1)}, u32[]{:S(2)}, u32[]{:S(2)}) collective-permute-start(bf16[2,2,3,48,384]{4,3,2,1,0:T(8,128)(2,1)S(1)} %pad_maximum_fusion.1.q_one), channel_id=1, source_target_pairs={{0,128},{1,129},{2,130},{3,131},{4,132},{5,133},{6,134},{7,135},{8... | collective-permute-start | bytes 1327112 | tf_op jit(solution)/shard_map/ppermute | solution.py:14
  120.5 16.4 %collective-permute-start.30 = (bf16[2,384,384]{2,1,0:T(8,128)(2,1)S(1)}, bf16[2,384,384]{2,1,0:T(8,128)(2,1)S(1)}, u32[]{:S(2)}, u32[]{:S(2)}) collective-permute-start(bf16[2,384,384]{2,1,0:T(8,128)(2,1)S(1)} %broadcast_select_fusion.2.across), channel_id=1, source_target_pairs={{0,1},{2,3},{4,5},{6,7},{8,9},{10,11},{12,13},{14,15},{16,17},{18,... | collective-permute-start | bytes 1769480 | tf_op jit(solution)/shard_map/ppermute | solution.py:14
  122.4 14.5 %collective-permute-start.24 = (bf16[2,2,3,48,384]{4,3,2,1,0:T(8,128)(2,1)S(1)}, bf16[2,2,3,48,384]{4,3,2,1,0:T(8,128)(2,1)S(1)}, u32[]{:S(2)}, u32[]{:S(2)}) collective-permute-start(bf16[2,2,3,48,384]{4,3,2,1,0:T(8,128)(2,1)S(1)} %pad_maximum_fusion.p_one), channel_id=1, source_target_pairs={{0,384},{1,385},{2,386},{3,387},{4,388},{5,389},{6,390},{7,391},{8... | collective-permute-start | bytes 1327112 | tf_op jit(solution)/shard_map/ppermute | solution.py:14
  (39 other events, 213.2 us)
